TPU v7x, 256 devices: a whole 4x4x8 slice. The times are simulated.
256 devices in a mesh: blk: 64 (over x, y_lo, z), dim: 4 (over y_hi, core).
Axes of the slice: x: 4, y: 4 (y_hi: 2, y_lo: 2; y = y_hi * 2 + y_lo), z: 8, core: 2. Of those that a mesh axis runs over, the one named last changes fastest.
Arguments:
- question_matrix: float32 [8192, 768], P('blk', 'dim'), may hold values from -20 to 20, as said below
- document_matrix: float32 [8192, 768], P('blk', 'dim'), may hold values from -0.5 to 0.5
- pool: float32 [768, 131072], P('dim', 'blk'), may hold values from -1.4 to 1.4
- hard_owner: int32 [8192, 8], P('blk'), may hold values from 0 to 63, all different within a row; in each aligned block of 128 rows (0 to 127, 128 to 255, ...) at most 32 rows name the same one
- hard_local: int32 [8192, 8], P('blk'), may hold values from 0 to 2047
Outputs:
- loss: float32 [8192], P('blk')
- question_derivative: float32 [8192, 768], P('blk', 'dim')
- document_derivative: float32 [8192, 768], P('blk', 'dim')
- grad_pool: float32 [768, 131072], P('dim', 'blk')
Inputs may be any that keep to these rules, and one draw needn't show every extreme that they name: `question_matrix`: query embeddings; some rows may be much larger than the rest. `hard_owner`: the 8 owners named in one row are different. Among the rows of one index of blk, no owner is named more than 32 times, a bound that some block reaches.
All inputs are finite; a program needn't handle non-finite values.
Results may differ from a plain program's by a relative error of at most 0.0003.
Values sent between devices are 32-bit elements; how exact they have to be, the bound alone decides.
A program may use at most 64 MiB of HBM per device.

v0:
```python
import jax
import jax.numpy as jnp
from jax import lax
from jax.sharding import PartitionSpec as P

logit_divisor = 0.05


def per_device(question_matrix, document_matrix, pool, hard_owner, hard_local):
    highest_accuracy = lax.Precision.HIGHEST
    blocks = lax.axis_size("blk")
    query_rows, feature_vectors = question_matrix.shape
    negatives = hard_owner.shape[1]
    capacity = min(query_rows, 2 * query_rows * negatives // blocks)
    owners = hard_owner.reshape(-1)
    local_rows = hard_local.reshape(-1)
    owner_marks = (owners[:, None] == jnp.arange(blocks, dtype=jnp.int32)[None, :]).astype(
        jnp.int32
    )
    slot_ranks = jnp.sum(jnp.cumsum(owner_marks, axis=0) * owner_marks, axis=1) - 1
    requests = jnp.zeros((blocks, capacity), jnp.int32).at[owners, slot_ranks].set(local_rows)
    asked = lax.all_to_all(requests, "blk", split_axis=0, concat_axis=0, tiled=True)
    found = jnp.moveaxis(jnp.take(pool, asked, axis=1), 0, 2)
    fetched = lax.all_to_all(found, "blk", split_axis=0, concat_axis=0, tiled=True)
    distractor_lines = fetched[owners, slot_ranks].reshape(query_rows, negatives, feature_vectors)
    hard_part = jnp.einsum(
        "pq,pcq->pc", question_matrix, distractor_lines, precision=highest_accuracy
    )
    positive_part = jnp.sum(question_matrix * document_matrix, axis=1)
    partial_value = lax.dot_general(
        question_matrix,
        lax.all_gather(document_matrix, "blk", axis=0, tiled=True),
        (((1,), (1,)), ((), ())),
        precision=highest_accuracy,
        preferred_element_type=jnp.float32,
    )
    gathered_lines, distractor_total, matching_logit_total = lax.psum(
        (partial_value, hard_part, positive_part), "dim"
    )
    affinity_logits = gathered_lines / logit_divisor
    distractor_logits = distractor_total / logit_divisor
    row_peak = jnp.maximum(jnp.max(affinity_logits, axis=1), jnp.max(distractor_logits, axis=1))
    summed = jnp.sum(jnp.exp(affinity_logits - row_peak[:, None]), axis=1) + jnp.sum(
        jnp.exp(distractor_logits - row_peak[:, None]), axis=1
    )
    normalizer_logarithm = row_peak + jnp.log(summed)
    softmax_rows = jnp.exp(affinity_logits - normalizer_logarithm[:, None])
    distractor_coefficients = jnp.exp(distractor_logits - normalizer_logarithm[:, None])
    objective_entries = normalizer_logarithm - matching_logit_total / logit_divisor
    distractor_addend = jnp.einsum(
        "jg,jgu->ju", distractor_coefficients, distractor_lines, precision=highest_accuracy
    )
    columns = softmax_rows
    replicated_lines = jnp.dot(
        columns,
        lax.all_gather(document_matrix, "blk", axis=0, tiled=True),
        precision=highest_accuracy,
        preferred_element_type=jnp.float32,
    )
    question_derivative = (replicated_lines + distractor_addend - document_matrix) / logit_divisor
    columns = softmax_rows
    received_lines = lax.psum_scatter(
        lax.dot_general(
            columns,
            question_matrix,
            (((0,), (0,)), ((), ())),
            precision=highest_accuracy,
            preferred_element_type=jnp.float32,
        ),
        "blk",
        scatter_dimension=0,
        tiled=True,
    )
    document_derivative = (received_lines - question_matrix) / logit_divisor
    dispatched_deltas = (
        distractor_coefficients[:, :, None] * question_matrix[:, None, :] / logit_divisor
    ).reshape(-1, feature_vectors)
    outgoing = (
        jnp.zeros((blocks, capacity, feature_vectors), jnp.float32)
        .at[owners, slot_ranks]
        .set(dispatched_deltas)
    )
    arriving = lax.all_to_all(outgoing, "blk", split_axis=0, concat_axis=0, tiled=True)
    grad_pool = (
        jnp.zeros(pool.shape, jnp.float32)
        .at[:, asked.reshape(-1)]
        .add(arriving.reshape(-1, feature_vectors).T)
    )
    return (objective_entries, question_derivative, document_derivative, grad_pool)


def solution(mesh):
    placed = (P("blk", "dim"), P("blk", "dim"), P("dim", "blk"), P("blk", None), P("blk", None))
    return jax.shard_map(
        per_device,
        mesh=mesh,
        in_specs=placed,
        out_specs=(P("blk"), P("blk", "dim"), P("blk", "dim"), P("dim", "blk")),
        check_vma=False,
    )
```

profile of v0, /device:TPU:16, one launch (start us, length us, event | category | flops | bytes accessed | tf_op | source)
XLA Modules:
  0.0 742.9 jit_solution(10958844967178127720)
XLA Ops:
  7.2 0.7 all-gather.2.cloned.1.call-update
  7.9 0.8 copy.24
  8.7 0.1 reshape.175
  9.0 18.0 %reduce-window.6 = s32[64,8,128]{2,1,0:T(8,128)S(1)} reduce-window(s32[64,8,128]{2,1,0:T(8,128)S(1)} %fusion.26, s32[]{:T(128)} %constant.20.clone.1), window={size=1x1x128 pad=0_0x0_0x127_0}, to_apply=%region_2.3 | reduce-window | flops 8323072 | bytes 524292 | tf_op jit(solution)/shard_map/reduce-window
  27.0 0.1 slice.12
  27.1 0.1 copy.27
  27.4 0.8 copy.29
  28.2 0.1 reshape.213
  28.3 0.1 broadcast_add_fusion
  28.6 0.8 and_reduce_fusion
  29.3 0.8 multiply_reduce_fusion.3
  30.1 4.3 scatter_custom_fusion.1
  34.5 0.7 copy.30
  35.2 12.7 %all-to-all-start = ((s32[64,1,32]{2,1,0:T(1,128)}), s32[64,1,32]{2,1,0:T(1,128)S(1)}, u32[]{:S(2)}, u32[]{:S(2)}) async-start(s32[64,1,32]{2,1,0:T(1,128)} %copy.30), calls=%async_computation | async-start | bytes 65536 | tf_op jit(solution)/shard_map/all_to_all | solution.py:22
  47.9 1.8 copy.31
  49.7 8.5 %all-to-all-done = s32[64,1,32]{2,1,0:T(1,128)S(1)} async-done(((s32[64,1,32]{2,1,0:T(1,128)}), s32[64,1,32]{2,1,0:T(1,128)S(1)}, u32[]{:S(2)}, u32[]{:S(2)}) %all-to-all-start) | async-done | bytes 8224 | tf_op jit(solution)/shard_map/all_to_all | solution.py:22
  58.3 209.4 %all-gather.2.cloned.1.call-done = f32[8192,192]{0,1:T(8,128)} async-done(((f32[128,192]{0,1:T(8,128)}), f32[8192,192]{0,1:T(8,128)}) %all-gather.2.cloned.1.call-update) | async-done | bytes 6291472 | tf_op jit(solution)/shard_map/all_gather | solution.py:32
  267.7 8.8 %fusion.31 = f32[128,8192]{1,0:T(8,128)} fusion(f32[128,192]{0,1:T(8,128)S(1)} %copy-done.1, f32[8192,192]{0,1:T(8,128)} %all-gather.2.cloned.1.call-done), kind=kOutput, calls=%fused_computation.67 | convolution fusion | flops 2415919104 | bytes 10584064 | tf_op jit(solution)/shard_map/dot_general | solution.py:30
  276.5 8.6 %gather_fusion = f32[2048,192]{1,0:T(8,128)} fusion(f32[192,2048]{0,1:T(8,128)S(1)} %copy.31, s32[2048]{0:T(1024)S(1)} %broadcast_clamp_fusion), kind=kCustom, calls=%fused_computation | custom fusion | bytes 3153920 | tf_op jit(solution)/shard_map/jit(_take)/gather | solution.py:23
  285.1 3.9 broadcast_select_fusion
  289.0 8.0 %all-to-all-start.1 = ((f32[64,32,192]{2,1,0:T(8,128)}), f32[64,32,192]{2,1,0:T(8,128)S(1)}, u32[]{:S(2)}, u32[]{:S(2)}) async-start(f32[64,32,192]{2,1,0:T(8,128)} %broadcast_select_fusion), calls=%async_computation.1 | async-start | bytes 4194304 | tf_op jit(solution)/shard_map/all_to_all | solution.py:24
  297.1 0.1 copy.34
  297.3 29.6 %all-to-all-done.1 = f32[64,32,192]{2,1,0:T(8,128)S(1)} async-done(((f32[64,32,192]{2,1,0:T(8,128)}), f32[64,32,192]{2,1,0:T(8,128)S(1)}, u32[]{:S(2)}, u32[]{:S(2)}) %all-to-all-start.1) | async-done | bytes 1572896 | tf_op jit(solution)/shard_map/all_to_all | solution.py:24
  326.8 7.3 gather_fusion.1
  334.1 1.1 fusion.16
  335.3 14.2 %all-reduce = (f32[128,8]{1,0:T(8,128)S(1)}, f32[128]{0:T(128)S(1)}) all-reduce(f32[128,8]{1,0:T(8,128)S(1)} %bitcast.60, f32[128]{0:T(128)S(1)} %multiply_reduce_fusion.1), channel_id=1, replica_groups=mesh['blk'=64,'dim'=4] {'dim'}, use_global_device_ids=true, to_apply=%region_6.7 | all-reduce | flops 1152 | bytes 9216 | tf_op jit(solution)/shard_map/psum | solution.py:37
  349.4 0.1 multiply_reduce_fusion.2
  349.5 31.4 %all-reduce.3.cloned.1.call-done = f32[128,8192]{1,0:T(8,128)} async-done(((f32[128,8192]{1,0:T(8,128)}), f32[128,8192]{1,0:T(8,128)}) %all-reduce.3.cloned.1.call-update) | async-done | bytes 4194320 | tf_op jit(solution)/shard_map/psum | solution.py:37
  381.0 2.7 multiply_reduce_fusion
  383.7 0.2 exponential_reduce_fusion.1
  383.9 0.6 copy-done
  384.4 0.8 exponential_reduce_fusion
  385.3 0.5 multiply_subtract_fusion
  385.8 7.8 %fusion = f32[8192,192]{0,1:T(8,128)} fusion(f32[128,192]{0,1:T(8,128)S(1)} %copy-done.1, f32[128,8192]{1,0:T(8,128)S(1)} %copy-done, f32[128]{0:T(128)S(1)} %get-tuple-element.21), kind=kOutput, calls=%fused_computation.7 | convolution fusion | flops 2418016256 | bytes 10584576 | tf_op jit(solution)/shard_map/dot_general | solution.py:63
  393.7 0.1 copy.32
  393.9 6.8 scatter_custom_fusion.2
  400.7 12.8 %all-to-all-start.2 = ((f32[64,32,192]{2,1,0:T(8,128)}), f32[64,32,192]{2,1,0:T(8,128)S(1)}, u32[]{:S(2)}, u32[]{:S(2)}) async-start(f32[64,32,192]{2,1,0:T(8,128)} %bitcast.19), calls=%async_computation.3 | async-start | bytes 4194304 | tf_op jit(solution)/shard_map/all_to_all | solution.py:83
  413.5 0.5 broadcast.194
  414.0 0.7 reduce.10
  414.8 1.0 fusion.14
  415.9 0.1 copy.37
  416.0 10.2 %fusion.10 = f32[128,192]{0,1:T(8,128)} fusion(f32[128,192]{0,1:T(8,128)S(1)} %copy-done.3, f32[8192,192]{0,1:T(8,128)} %all-gather.2.cloned.1.call-done, f32[128,8192]{1,0:T(8,128)} %all-reduce.3.cloned.1.call-done, f32[128]{0:T(128)S(1)} %get-tuple-element.21, f32[128,1,192]{0,2,1:T(8,128)S(1)} %copy.37), kind=kOutput, calls=%fused_computation.18 | convolution fusion | flops 2418089984 | bytes 10781184 | tf_op jit(solution)/shard_map/dot_general | solution.py:54
  426.2 48.6 %all-to-all-done.2 = f32[64,32,192]{2,1,0:T(8,128)S(1)} async-done(((f32[64,32,192]{2,1,0:T(8,128)}), f32[64,32,192]{2,1,0:T(8,128)S(1)}, u32[]{:S(2)}, u32[]{:S(2)}) %all-to-all-start.2) | async-done | bytes 1572896 | tf_op jit(solution)/shard_map/all_to_all | solution.py:83
  474.8 1.3 copy-done.2
  476.1 12.5 %scatter_custom_fusion = f32[192,2048]{0,1:T(8,128)S(1)} fusion(s32[2048]{0:T(1024)S(1)} %bitcast.65, f32[2048,192]{1,0:T(8,128)} %bitcast.55, f32[]{:T(128)} %constant.50.clone.1), kind=kCustom, calls=%fused_computation.28 | custom fusion | flops 393216 | bytes 1573376 | tf_op jit(solution)/shard_map/scatter-add | solution.py:87
  488.6 1.7 copy.33
  490.3 244.5 %reduce-scatter.2.cloned.1.call-done = f32[128,192]{0,1:T(8,128)} async-done(((f32[8192,192]{0,1:T(8,128)}), f32[128,192]{0,1:T(8,128)}) %reduce-scatter.2.cloned.1.call-update) | async-done | bytes 98320 | tf_op jit(solution)/shard_map/reduce_scatter | solution.py:62
  734.8 1.5 subtract_multiply_fusion
  (32 shorter events, 1.1 us)
Async XLA Ops:
  7.2 260.5 %copy-start.1 = (f32[128,192]{0,1:T(8,128)S(1)}, f32[128,192]{0,1:T(8,128)}, u32[]{:S(2)}) copy-start(f32[128,192]{0,1:T(8,128)} %param.5) | copy-start | bytes 294916
  7.2 260.5 %all-gather.2.cloned.1.call-start = ((), (), s32[]{:S(2)}) async-start(), calls=%async_computation.4 | async-start | bytes 6389760 | tf_op jit(solution)/shard_map/all_gather | solution.py:32
  35.2 23.0 %all-to-all-start = ((s32[64,1,32]{2,1,0:T(1,128)}), s32[64,1,32]{2,1,0:T(1,128)S(1)}, u32[]{:S(2)}, u32[]{:S(2)}) async-start(s32[64,1,32]{2,1,0:T(1,128)} %copy.30), calls=%async_computation | async-start | bytes 65536 | tf_op jit(solution)/shard_map/all_to_all | solution.py:22
  47.9 333.1 %all-reduce.3.cloned.1.call-start = ((), (), s32[]{:S(2)}) async-start(), calls=%async_computation.5 | async-start | bytes 8388608 | tf_op jit(solution)/shard_map/psum | solution.py:37
  285.1 12.1 %copy-start.3 = (f32[128,192]{0,1:T(8,128)S(1)}, f32[128,192]{0,1:T(8,128)}, u32[]{:S(2)}) copy-start(f32[128,192]{0,1:T(8,128)} %param.6) | copy-start | bytes 294916
  289.0 37.8 %all-to-all-start.1 = ((f32[64,32,192]{2,1,0:T(8,128)}), f32[64,32,192]{2,1,0:T(8,128)S(1)}, u32[]{:S(2)}, u32[]{:S(2)}) async-start(f32[64,32,192]{2,1,0:T(8,128)} %broadcast_select_fusion), calls=%async_computation.1 | async-start | bytes 4194304 | tf_op jit(solution)/shard_map/all_to_all | solution.py:24
  297.0 437.8 %reduce-scatter.2.cloned.1.call-start = ((), (), s32[]{:S(2)}) async-start(), calls=%async_computation.6 | async-start | bytes 6389760 | tf_op jit(solution)/shard_map/reduce_scatter | solution.py:62
  381.0 3.4 copy-start
  400.7 74.1 %all-to-all-start.2 = ((f32[64,32,192]{2,1,0:T(8,128)}), f32[64,32,192]{2,1,0:T(8,128)S(1)}, u32[]{:S(2)}, u32[]{:S(2)}) async-start(f32[64,32,192]{2,1,0:T(8,128)} %bitcast.19), calls=%async_computation.3 | async-start | bytes 4194304 | tf_op jit(solution)/shard_map/all_to_all | solution.py:83
  474.8 1.4 copy-start.2
Sparse Core Ops, SparseCore 0:
  9.7 257.8 all-gather.1
  276.6 104.2 all-reduce.2
  393.8 341.0 reduce-scatter.1
where the time goes:
time: 743 us
  waiting for transfers between devices  573 us (77%)
  other arithmetic  49.7 us (7%)
  starting transfers between devices  33.5 us (5%)
  local copies, waits for them, and re-layouts  29.8 us (4%)
  matrix products  29 us (4%)
  blocking collectives  14.2 us (2%)
  between operations  14 us (2%)
    reduce_scatter x1, waiting for transfers between devices, per_device(): lax.psum_scatter(lax.dot_general(columns, question_matrix, (((0,), (0,)),...  245 us
    all_gather x1, waiting for transfers between devices, per_device(): lax.all_gather(document_matrix, 'blk', axis=0, tiled=True)  209 us
    all_to_all x1, waiting for transfers between devices, per_device(): lax.all_to_all(outgoing, 'blk', split_axis=0, concat_axis=0, tiled=True)  48.6 us
    psum x1, waiting for transfers between devices, per_device(): lax.psum((partial_value, hard_part, positive_part), 'dim')  31.4 us
    all_to_all x1, waiting for transfers between devices, per_device(): lax.all_to_all(found, 'blk', split_axis=0, concat_axis=0, tiled=True)  29.6 us
    another operation x3, other arithmetic  18.2 us
  transfers between devices with their start and end apart: 6, of which 6 were waited for; matrix products, arithmetic and copies ran while one was open for 11% of the time, Pallas kernels for 0%

commit v1 on v0

v1 whole, which is shorter than its diff:
```python
import jax
import jax.numpy as jnp
from jax import lax
from jax.experimental import pallas as pl
from jax.experimental.pallas import tpu as pltpu
from jax.sharding import PartitionSpec as P

MESH = pl.DeviceIdType.MESH
F32 = jnp.float32
BF16 = jnp.bfloat16
HIGHEST = lax.Precision.HIGHEST
SCALE = 20.0

NT = (((1,), (1,)), ((), ()))
NN = (((1,), (0,)), ((), ()))


def mm(a, b, dims, precision=None):
    return lax.dot_general(a, b, dims, precision=precision, preferred_element_type=F32)


def split3(x):
    high = x.astype(BF16)
    rest = x - high.astype(F32)
    mid = rest.astype(BF16)
    low = (rest - mid.astype(F32)).astype(BF16)
    return high, mid, low


def loop(count, body):
    def step(i, carry):
        body(i)
        return carry

    lax.fori_loop(0, count, step, 0)


REQ, DOC, ROWS, QUERY, DGRAD, PROB = range(6)
SIB_D, SIB_Q, SIB_H, SIB_G, SIB_DD, PART_Q, PART_DQ, PART_L = range(8)


def kernel(
    q_ref, d_ref, pool_ref, idx_ref,
    loss_ref, dq_ref, dd_ref, gp_ref,
    idx_all, q_all, d_mine, d_all, lr_all, sid, rq_out, rq_in, lt, pool_s,
    p_out, p_in, f_out, f_in, hs_mine, hs_sib, hq, st, ch, stat_out, stat_in,
    hc_out, hc_in, g3_out, g3_in, dd_sib, g_sib_out, g_sib_in, g_out, g_in, wcat, at_s,
    dq_out, dq_in, loss_out, loss_in, dd_out, lrow,
    plane_s, plane_r, row_s, row_r, idx_s, idx_r, qs, qr, gs, gr, one_s, one_r,
):
    blk, dim = lax.axis_index("blk"), lax.axis_index("dim")
    xy, z = blk // 8, blk % 8
    yh, c = dim // 2, dim % 2
    t = z // 2
    holder = (z % 2) == yh
    me_p = xy * 2 + yh
    me_r = z * 2 + c

    def plane_dev(p):
        return ((p // 2) * 8 + z, (p % 2) * 2 + c)

    def row_dev(r):
        return (xy * 8 + r // 2, yh * 2 + r % 2)

    def z_dev(zz):
        return (xy * 8 + zz, dim)

    sibling = (blk, yh * 2 + (1 - c))
    partner = (blk, (1 - yh) * 2 + c)

    def remote(src, dst, send, recv, device):
        return pltpu.make_async_remote_copy(
            src_ref=src, dst_ref=dst, send_sem=send, recv_sem=recv,
            device_id=device, device_id_type=MESH,
        )

    def plane(phase, src, dst_here, dst_there, p, slot):
        return remote(src, dst_there, plane_s.at[phase, p], plane_r.at[phase, slot], plane_dev(p))

    barrier = pltpu.get_barrier_semaphore()

    def greet(k):
        pl.semaphore_signal(barrier, inc=1, device_id=plane_dev((me_p + k + 1) % 16), device_id_type=MESH)
        pl.semaphore_signal(barrier, inc=1, device_id=row_dev((me_r + k + 1) % 16), device_id_type=MESH)

    loop(15, greet)
    pl.semaphore_wait(barrier, 30)

    def idx_copy(zz):
        return remote(idx_ref, idx_all.at[t], idx_s.at[zz], idx_r.at[t], z_dev(zz))

    def q_copy(part, zz):
        return remote(
            q_all.at[c, part, t], q_all.at[c, part, t], qs.at[part, zz], qr.at[part, t], z_dev(zz)
        )

    sib_d = remote(
        d_ref.at[pl.ds((1 - c) * 64, 64)], d_mine.at[c], one_s.at[SIB_D], one_r.at[SIB_D], sibling
    )
    part_q = remote(q_ref, q_all.at[c, yh, t], one_s.at[PART_Q], qr.at[yh, t], partner)
    part_q_in = remote(q_ref, q_all.at[c, 1 - yh, t], one_s.at[PART_Q], qr.at[1 - yh, t], partner)

    @pl.when(holder)
    def _():
        def send(k):
            idx_copy((z + k + 1) % 8).start()

        loop(7, send)

    sib_d.start()

    @pl.when(jnp.logical_not(holder))
    def _():
        part_q.start()

    @pl.when(holder)
    def _():
        q_all[c, yh, t] = q_ref[...]
        idx_all[t] = idx_ref[...]

        def send(k):
            q_copy(yh, (z + k + 1) % 8).start()

        loop(7, send)

    d_mine[c] = d_ref[pl.ds(pl.multiple_of(c * 64, 64), 64), :]
    d_all[yh, c, xy] = d_ref[pl.ds(pl.multiple_of(c * 64, 64), 64), :]
    sib_d.wait_recv()

    def doc_copy(p, slot):
        return remote(
            d_mine, d_all.at[slot % 2, :, slot // 2],
            plane_s.at[DOC, p], plane_r.at[DOC, slot], plane_dev(p),
        )

    loop(15, lambda k: doc_copy((me_p + k + 1) % 16, me_p).start())
    d_all[yh, 1 - c, xy] = d_mine[1 - c]

    def idx_wait(tt):
        @pl.when(2 * tt + yh != z)
        def _():
            remote(idx_ref, idx_all.at[tt], idx_s.at[0], idx_r.at[tt], partner).wait_recv()

    loop(4, idx_wait)
    sub8 = lax.broadcasted_iota(jnp.int32, (8, 128), 0)
    upper = jnp.where(
        lax.broadcasted_iota(jnp.int32, (128, 128), 0) < lax.broadcasted_iota(jnp.int32, (128, 128), 1),
        1.0, 0.0,
    ).astype(BF16)
    for tt in range(4):
        owner = idx_all[tt, 0:8]
        local = idx_all[tt, 8:16] + 1
        table = jnp.zeros((8, 128), jnp.int32)
        for a in range(8):
            row = jnp.sum(jnp.where(owner == a * 8 + z, local, 0), axis=0, keepdims=True)
            table = jnp.where(sub8 == a, row, table)
        marks = jnp.where(table > 0, 1.0, 0.0)
        rank = mm(marks.astype(BF16), upper, NN)
        lr_all[:, tt * 128 : (tt + 1) * 128] = table.astype(F32)
        sid[:, tt * 128 : (tt + 1) * 128] = jnp.where(table > 0, rank + float(tt * 32), -1.0)

    sub512 = lax.broadcasted_iota(jnp.int32, (128, 512), 0).astype(F32)
    lane128 = lax.broadcasted_iota(jnp.int32, (128, 128), 1)

    def hot(a):
        return sub512 == sid[pl.ds(a, 1), :]

    def columns(rows):
        def step(a, table):
            col = jnp.sum(jnp.where(hot(a), rows[pl.ds(a, 1), :], 0.0), axis=1, keepdims=True)
            return jnp.where(lane128 == a, col, table)

        return lax.fori_loop(0, 8, step, jnp.zeros((128, 128), F32))

    wanted = columns(lr_all).T
    for a in range(8):
        rq_out[a] = wanted[a : a + 1, :]
    rq_in[me_p] = rq_out[xy]

    def req_copy(p, slot):
        return remote(
            rq_out.at[p // 2], rq_in.at[slot], plane_s.at[REQ, p], plane_r.at[REQ, slot], plane_dev(p)
        )

    loop(15, lambda k: req_copy((me_p + k + 1) % 16, me_p).start())

    @pl.when(holder)
    def _():
        part_q_in.wait_recv()
        loop(7, lambda k: q_copy(1 - yh, (z + k + 1) % 8).start())

    for k, part in enumerate(split3(pool_ref[...])):
        pool_s[k] = part

    def req_wait(k):
        p = (me_p + k + 1) % 16
        req_copy(p, p).wait_recv()

    loop(15, req_wait)
    named = jnp.concatenate([rq_in[i] for i in range(16)] + [jnp.zeros((112, 128), F32)], axis=0)
    lt[...] = named.T
    lane2048 = lax.broadcasted_iota(jnp.int32, (128, 2048), 1).astype(F32) + 1.0

    def rows_copy(p, slot):
        return remote(
            p_out.at[p], p_in.at[slot % 2, slot // 2],
            plane_s.at[ROWS, p], plane_r.at[ROWS, slot], plane_dev(p),
        )

    def fetch(g):
        hots = []
        for i in range(4):
            col = jnp.sum(jnp.where(lane128 == g * 4 + i, lt[...], 0.0), axis=1, keepdims=True)
            hots.append(jnp.where(col == lane2048, 1.0, 0.0).astype(BF16))
        hots = jnp.concatenate(hots, axis=0)
        got = mm(hots, pool_s[0], NT) + mm(hots, pool_s[1], NT) + mm(hots, pool_s[2], NT)
        for i in range(4):
            p = g * 4 + i
            p_out[p] = got[i * 128 : (i + 1) * 128]

            @pl.when(p != me_p)
            def _():
                rows_copy(p, me_p).start()

    loop(4, fetch)
    p_in[yh, xy] = p_out[me_p]

    def q_wait(tt):
        @pl.when(2 * tt + yh != z)
        def _():
            for part in range(2):
                remote(
                    q_ref, q_all.at[c, part, tt], one_s.at[PART_Q], qr.at[part, tt], partner
                ).wait_recv()

    loop(4, q_wait)
    sib_q = remote(q_all.at[c], q_all.at[c], one_s.at[SIB_Q], one_r.at[SIB_Q], sibling)
    sib_q.start()

    def query_copy(p, slot):
        return remote(
            f_out.at[p], f_in.at[slot], plane_s.at[QUERY, p], plane_r.at[QUERY, slot], plane_dev(p)
        )

    for part in range(2):
        queries = split3(q_all[c, part].reshape(512, 192))

        def pick(g):
            hots = jnp.concatenate(
                [jnp.where(hot(g * 4 + i), 1.0, 0.0).astype(BF16) for i in range(4)], axis=0
            )
            got = mm(hots, queries[0], NN) + mm(hots, queries[1], NN) + mm(hots, queries[2], NN)
            for i in range(4):
                p = (g * 4 + i) * 2 + part
                f_out[p] = got[i * 128 : (i + 1) * 128]

                @pl.when(p != me_p)
                def _():
                    query_copy(p, me_p).start()

        loop(2, pick)
    f_in[me_p] = f_out[me_p]

    remote(q_all.at[c], q_all.at[1 - c], one_s.at[SIB_Q], one_r.at[SIB_Q], sibling).wait_recv()

    def doc_wait(k):
        p = (me_p + k + 1) % 16
        doc_copy(p, p).wait_recv()

    loop(15, doc_wait)

    def score(j):
        total = None
        for part in range(2):
            for core in range(2):
                docs = d_all[part, core, pl.ds(j * 4, 4)].reshape(256, 192)
                value = mm(docs, q_all[core, part].reshape(512, 192), NT, HIGHEST)
                total = value if total is None else total + value
        st[pl.ds(pl.multiple_of(j * 256, 256), 256), :] = total * SCALE

    loop(2, score)

    def rows_wait(k):
        p = (me_p + k + 1) % 16
        rows_copy(p, p).wait_recv()

    loop(15, rows_wait)

    def hard_part(a, table):
        col = jnp.sum(
            p_in[0, a] * f_out[a * 2] + p_in[1, a] * f_out[a * 2 + 1], axis=1, keepdims=True
        )
        return jnp.where(lane128 == a, col, table)

    hs_mine[...] = lax.fori_loop(0, 8, hard_part, jnp.zeros((128, 128), F32))
    sib_h = remote(hs_mine, hs_sib, one_s.at[SIB_H], one_r.at[SIB_H], sibling)
    sib_h.start()

    def top(j, best):
        rows = st[pl.ds(pl.multiple_of(j * 64, 64), 64), :].reshape(8, 8, 512)
        return jnp.maximum(best, jnp.max(rows, axis=0))

    best = lax.fori_loop(0, 8, top, jnp.full((8, 512), -jnp.inf, F32))
    best = jnp.max(best, axis=0, keepdims=True)
    sib_h.wait_recv()
    hard = (hs_mine[...] + hs_sib[...]) * SCALE
    for a in range(8):
        row = jnp.sum(jnp.where(hot(a), hard[:, a : a + 1], 0.0), axis=0, keepdims=True)
        hq[a : a + 1, :] = jnp.where(sid[a : a + 1, :] >= 0.0, row, -jnp.inf)
    peak = jnp.maximum(best, jnp.max(hq[...], axis=0, keepdims=True))

    def add(j, total):
        rows = jnp.exp(st[pl.ds(pl.multiple_of(j * 64, 64), 64), :] - peak)
        return total + jnp.sum(rows.reshape(8, 8, 512), axis=0)

    total = lax.fori_loop(0, 8, add, jnp.zeros((8, 512), F32))
    total = total + jnp.exp(hq[...] - peak) * jnp.where(c == 0, 1.0, 0.0)
    total = jnp.sum(total, axis=0, keepdims=True)
    square = st[pl.ds(pl.multiple_of(xy * 64, 64), 64), pl.ds(pl.multiple_of(t * 128, 128), 128)]
    on_diagonal = lax.broadcasted_iota(jnp.int32, (64, 128), 1) == (
        lax.broadcasted_iota(jnp.int32, (64, 128), 0) + c * 64
    )
    positive = jnp.sum(jnp.where(on_diagonal, square, 0.0), axis=0, keepdims=True)
    positive = positive * jnp.where(holder, 1.0, 0.0)
    positive = jnp.concatenate([positive] * 4, axis=1)
    here = lax.broadcasted_iota(jnp.int32, (1, 512), 1) // 128 == t
    positive = jnp.where(here, positive, 0.0)
    sub8w = lax.broadcasted_iota(jnp.int32, (8, 512), 0)
    stat_out[...] = jnp.where(sub8w == 0, peak, jnp.where(sub8w == 1, total, positive))
    stat_in[me_r] = stat_out[...]

    def stat_copy(r, slot):
        return remote(stat_out, stat_in.at[slot], row_s.at[r], row_r.at[slot], row_dev(r))

    loop(15, lambda k: stat_copy((me_r + k + 1) % 16, me_r).start())

    def stat_wait(k):
        r = (me_r + k + 1) % 16
        stat_copy(r, r).wait_recv()

    loop(15, stat_wait)
    peak = stat_in[0, 0:1, :]
    for r in range(1, 16):
        peak = jnp.maximum(peak, stat_in[r, 0:1, :])
    total = jnp.zeros((1, 512), F32)
    positive = jnp.zeros((1, 512), F32)
    for r in range(16):
        total = total + stat_in[r, 1:2, :] * jnp.exp(stat_in[r, 0:1, :] - peak)
        positive = positive + stat_in[r, 2:3, :]
    log_total = peak + jnp.log(total)
    lrow[...] = log_total - positive

    hcq = jnp.exp(hq[...] - log_total)
    hq[...] = hcq
    chances = columns(hq).T
    for a in range(8):
        hc_out[a] = chances[a : a + 1, :]
    hc_in[me_p] = hc_out[xy]

    def prob_copy(p, slot):
        return remote(
            hc_out.at[p // 2], hc_in.at[slot], plane_s.at[PROB, p], plane_r.at[PROB, slot], plane_dev(p)
        )

    loop(15, lambda k: prob_copy((me_p + k + 1) % 16, me_p).start())

    def chance(j):
        rows = pl.ds(pl.multiple_of(j * 64, 64), 64)
        st[rows, :] = jnp.exp(st[rows, :] - log_total)

    loop(8, chance)

    def doc_grad(k):
        part, core = k // 2, k % 2
        value = mm(st[...], q_all[core, part].reshape(512, 192), NN, HIGHEST)
        g3_out[:, part, core] = value.reshape(8, 64, 192)

    loop(4, doc_grad)

    def dgrad_copy(p, slot):
        return remote(
            g3_out.at[p // 2, p % 2], g3_in.at[slot],
            plane_s.at[DGRAD, p], plane_r.at[DGRAD, slot], plane_dev(p),
        )

    loop(15, lambda k: dgrad_copy((me_p + k + 1) % 16, me_p).start())
    g3_in[me_p] = g3_out[xy, yh]

    ch[...] = st[...].T

    def query_grad_sib(part):
        g_sib_out[part] = mm(ch[...], d_all[part, 1 - c].reshape(512, 192), NN, HIGHEST)

    loop(2, query_grad_sib)
    sib_g = remote(g_sib_out, g_sib_in, one_s.at[SIB_G], one_r.at[SIB_G], sibling)
    sib_g.start()

    filler = jnp.zeros((120, 512), F32)
    sid_t = jnp.concatenate([sid[...], filler], axis=0).T
    hc_t = jnp.concatenate([hq[...], filler], axis=0).T
    lane512 = lax.broadcasted_iota(jnp.int32, (512, 128), 1).astype(F32)
    for a in range(8):
        wcat[:, a * 128 : (a + 1) * 128] = jnp.where(
            sid_t[:, a : a + 1] == lane512, hc_t[:, a : a + 1], 0.0
        )

    def query_grad(part):
        value = mm(ch[...], d_all[part, c].reshape(512, 192), NN, HIGHEST)
        value = value + mm(wcat[...], p_in[part].reshape(1024, 192), NN, HIGHEST)
        g_out[:, part] = value.reshape(4, 128, 192)

    loop(2, query_grad)
    sib_g.wait_recv()
    for part in range(2):
        g_out[:, part] += g_sib_in[part].reshape(4, 128, 192)

    def grad_copy(tt, slot):
        return remote(g_out.at[tt], g_in.at[slot], gs.at[tt], gr.at[slot], z_dev(2 * tt + yh))

    def grad_send(tt):
        @pl.when(2 * tt + yh != z)
        def _():
            grad_copy(tt, z).start()

    loop(4, grad_send)

    @pl.when(holder)
    def _():
        g_in[z] = g_out[t]

    def query_wait(k):
        p = (me_p + k + 1) % 16
        query_copy(p, p).wait_recv()
        prob_copy(p, p).wait_recv()

    loop(15, query_wait)
    chances = jnp.concatenate([hc_in[i] for i in range(16)] + [jnp.zeros((112, 128), F32)], axis=0).T

    def turn(i):
        col = jnp.sum(jnp.where(lane128 == i, chances, 0.0), axis=1, keepdims=True)
        terms = split3((f_in[i] * (col * SCALE)).T)
        for k in range(3):
            at_s[k, :, pl.ds(pl.multiple_of(i * 128, 128), 128)] = terms[k]

    loop(16, turn)
    lane256 = lax.broadcasted_iota(jnp.int32, (128, 256), 1).astype(F32) + 1.0

    def pool_grad(n):
        base = (n * 256).astype(F32)
        hots = jnp.concatenate(
            [
                jnp.where(lt[:, i : i + 1] == lane256 + base, 1.0, 0.0).astype(BF16)
                for i in range(16)
            ],
            axis=0,
        )
        value = mm(at_s[0], hots, NN) + mm(at_s[1], hots, NN) + mm(at_s[2], hots, NN)
        gp_ref[:, pl.ds(pl.multiple_of(n * 256, 256), 256)] = value

    loop(8, pool_grad)

    def dgrad_wait(k):
        p = (me_p + k + 1) % 16
        dgrad_copy(p, p).wait_recv()

    loop(15, dgrad_wait)

    def sum_docs(core):
        value = g3_in[0, core]
        for p in range(1, 16):
            value = value + g3_in[p, core]
        return value

    dd_out[...] = sum_docs(1 - c)
    sib_dd = remote(dd_out, dd_sib, one_s.at[SIB_DD], one_r.at[SIB_DD], sibling)
    sib_dd.start()
    mine = pl.ds(pl.multiple_of(c * 64, 64), 64)
    dd_ref[mine, :] = (sum_docs(c) - q_ref[mine, :]) * SCALE

    part_dq = remote(dq_out, dq_in, one_s.at[PART_DQ], one_r.at[PART_DQ], partner)
    part_l = remote(loss_out, loss_in, one_s.at[PART_L], one_r.at[PART_L], partner)

    @pl.when(holder)
    def _():
        loss_out[...] = lrow[:, pl.ds(pl.multiple_of(t * 128, 128), 128)]
        part_l.start()

        def wait(k):
            zz = (z + k + 1) % 8
            grad_copy(t, zz).wait_recv()

        loop(7, wait)

        def sum_queries(part):
            value = g_in[0, part]
            for zz in range(1, 8):
                value = value + g_in[zz, part]
            return value

        dq_out[...] = sum_queries(1 - yh)
        part_dq.start()
        dq_ref[...] = (sum_queries(yh) - d_ref[...]) * SCALE
        loss_ref[...] = loss_out[...]

    @pl.when(jnp.logical_not(holder))
    def _():
        part_l.wait_recv()
        loss_ref[...] = loss_in[...]
        part_dq.wait_recv()
        dq_ref[...] = (dq_in[...] - d_ref[...]) * SCALE

    sib_dd.wait_recv()
    other = pl.ds(pl.multiple_of((1 - c) * 64, 64), 64)
    dd_ref[other, :] = (dd_sib[...] - q_ref[other, :]) * SCALE

    sib_d.wait_send()
    sib_q.wait_send()
    sib_h.wait_send()
    sib_g.wait_send()
    sib_dd.wait_send()

    def sent(k):
        p = (me_p + k + 1) % 16
        for copy in (doc_copy, req_copy, rows_copy, query_copy, prob_copy, dgrad_copy):
            copy(p, me_p).wait_send()
        stat_copy((me_r + k + 1) % 16, me_r).wait_send()

    loop(15, sent)

    def grad_sent(tt):
        @pl.when(2 * tt + yh != z)
        def _():
            grad_copy(tt, z).wait_send()

    loop(4, grad_sent)

    @pl.when(holder)
    def _():
        def z_sent(k):
            zz = (z + k + 1) % 8
            idx_copy(zz).wait_send()
            q_copy(yh, zz).wait_send()
            q_copy(1 - yh, zz).wait_send()

        loop(7, z_sent)
        part_l.wait_send()
        part_dq.wait_send()

    @pl.when(jnp.logical_not(holder))
    def _():
        part_q.wait_send()


def per_device(question_matrix, document_matrix, pool, hard_owner, hard_local):
    index = jnp.concatenate([hard_owner.T, hard_local.T], axis=0)
    vmem = pl.BlockSpec(memory_space=pltpu.VMEM)
    f = lambda *shape: pltpu.VMEM(shape, F32)
    scratch = [
        pltpu.VMEM((4, 16, 128), jnp.int32),
        f(2, 2, 4, 128, 192),
        f(2, 64, 192),
        f(2, 2, 8, 64, 192),
        f(8, 512),
        f(8, 512),
        f(8, 1, 128),
        f(16, 1, 128),
        f(128, 128),
        pltpu.VMEM((3, 192, 2048), BF16),
        f(16, 128, 192),
        f(2, 8, 128, 192),
        f(16, 128, 192),
        f(16, 128, 192),
        f(128, 128),
        f(128, 128),
        f(8, 512),
        f(512, 512),
        f(512, 512),
        f(8, 512),
        f(16, 8, 512),
        f(8, 1, 128),
        f(16, 1, 128),
        f(8, 2, 2, 64, 192),
        f(16, 2, 64, 192),
        f(64, 192),
        f(2, 512, 192),
        f(2, 512, 192),
        f(4, 2, 128, 192),
        f(8, 2, 128, 192),
        f(512, 1024),
        pltpu.VMEM((3, 192, 2048), BF16),
        f(128, 192),
        f(128, 192),
        f(1, 128),
        f(1, 128),
        f(64, 192),
        f(1, 512),
        pltpu.SemaphoreType.DMA((6, 16)),
        pltpu.SemaphoreType.DMA((6, 16)),
        pltpu.SemaphoreType.DMA((16,)),
        pltpu.SemaphoreType.DMA((16,)),
        pltpu.SemaphoreType.DMA((8,)),
        pltpu.SemaphoreType.DMA((4,)),
        pltpu.SemaphoreType.DMA((2, 8)),
        pltpu.SemaphoreType.DMA((2, 4)),
        pltpu.SemaphoreType.DMA((4,)),
        pltpu.SemaphoreType.DMA((8,)),
        pltpu.SemaphoreType.DMA((8,)),
        pltpu.SemaphoreType.DMA((8,)),
    ]
    loss, dq, dd, gp = pl.pallas_call(
        kernel,
        name="retriever_step",
        out_shape=(
            jax.ShapeDtypeStruct((1, 128), F32),
            jax.ShapeDtypeStruct((128, 192), F32),
            jax.ShapeDtypeStruct((128, 192), F32),
            jax.ShapeDtypeStruct((192, 2048), F32),
        ),
        in_specs=[vmem] * 4,
        out_specs=(vmem,) * 4,
        scratch_shapes=scratch,
        compiler_params=pltpu.CompilerParams(
            collective_id=0, has_side_effects=True, vmem_limit_bytes=60 * 1024 * 1024
        ),
    )(question_matrix, document_matrix, pool, index)
    return loss.reshape(128), dq, dd, gp


def solution(mesh):
    placed = (P("blk", "dim"), P("blk", "dim"), P("dim", "blk"), P("blk", None), P("blk", None))
    return jax.shard_map(
        per_device,
        mesh=mesh,
        in_specs=placed,
        out_specs=(P("blk"), P("blk", "dim"), P("blk", "dim"), P("dim", "blk")),
        check_vma=False,
    )
```

time: 743 us -> 182 us (0.24)
  the two profiles are of different devices: /device:TPU:16 before, /device:TPU:84 now
where the time goes in v1:
time: 182 us; the launch traced here: 181 us
  Pallas kernels  169 us (93%)
  local copies, waits for them, and re-layouts  10.5 us (6%)
    pallas_call x1, Pallas kernels, per_device(): pl.pallas_call(kernel, name='retriever_step', out_shape=(jax.ShapeDtypeSt...  169 us
    unnamed x6, local copies, waits for them, and re-layouts  10.5 us

profile of v1, /device:TPU:84, one launch (start us, length us, event | category | flops | bytes accessed | tf_op | source)
XLA Modules:
  0.0 181.3 jit_solution(9120288750138126381)
XLA Ops:
  0.6 1.3 pad_add_fusion.idx_ref
  1.9 1.6 copy.9.q_ref
  3.6 1.6 copy.10.d_ref
  5.2 168.9 %retriever_step.1 = (f32[1,128]{1,0:T(1,128)}, f32[128,192]{1,0:T(8,128)}, f32[128,192]{1,0:T(8,128)}, f32[192,2048]{1,0:T(8,128)}) custom-call(f32[128,192]{1,0:T(8,128)} %copy.9.q_ref, f32[128,192]{1,0:T(8,128)} %copy.10.d_ref, f32[192,2048]{1,0:T(8,128)} %pool_ref.1, s32[16,128]{1,0:T(8,128)} %pad_add_fusion.idx_ref), custom_call_target="tpu_custom_call" | custom-call | tf_op jit(solution)/shard_map/retriever_step/pallas_call | solution.py:610
  174.1 1.6 copy.11
  175.8 1.6 copy.12
  177.4 1.2 copy.15
  178.6 2.7 %copy.16 = f32[192,2048]{1,0:T(8,128)} copy(f32[192,2048]{1,0:T(8,128)} %get-tuple-element.23) | data formatting | bytes 3145728

commit v2 on v1

v2 whole, which is shorter than its diff:
```python
import jax
import jax.numpy as jnp
from jax import lax
from jax.experimental import pallas as pl
from jax.experimental.pallas import tpu as pltpu
from jax.sharding import PartitionSpec as P

MESH = pl.DeviceIdType.MESH
F32 = jnp.float32
BF16 = jnp.bfloat16
HIGHEST = lax.Precision.HIGHEST
SCALE = 20.0

NT = (((1,), (1,)), ((), ()))
NN = (((1,), (0,)), ((), ()))


def mm(a, b, dims, precision=None):
    return lax.dot_general(a, b, dims, precision=precision, preferred_element_type=F32)


def split3(x):
    high = x.astype(BF16)
    rest = x - high.astype(F32)
    mid = rest.astype(BF16)
    low = (rest - mid.astype(F32)).astype(BF16)
    return high, mid, low


def loop(count, body):
    def step(i, carry):
        body(i)
        return carry

    lax.fori_loop(0, count, step, 0)


def halves(x):
    return x[:, :128], x[:, 128:256], x[:, 256:384]


def low(rows):
    return lax.broadcasted_iota(jnp.int32, (rows, 128), 1) < 64


def turned(x):
    return pltpu.roll(x, 64, 1)


def fold(a, b):
    keep = low(a.shape[0])
    b0, b1 = turned(b[:, :128]), turned(b[:, 128:256])
    return jnp.concatenate(
        [a[:, :128], jnp.where(keep, a[:, 128:256], b0), jnp.where(keep, b0, b1)], axis=1
    )


def unfold(x):
    x0, x1, x2 = halves(x)
    x1t, x2t = turned(x1), turned(x2)
    return (
        jnp.concatenate([x0, x1], axis=1),
        jnp.concatenate([jnp.where(low(x.shape[0]), x1t, x2t), x2t], axis=1),
    )


def regroup(x, y):
    x0, x1, x2 = halves(x)
    y0, y1, y2 = halves(y)
    keep = low(x.shape[0])
    x1t, x2t, y0t, y1t = turned(x1), turned(x2), turned(y0), turned(y1)
    first = jnp.concatenate([x0, jnp.where(keep, x1, y0t), jnp.where(keep, y0t, y1t)], axis=1)
    last = jnp.concatenate([jnp.where(keep, x1t, x2t), jnp.where(keep, x2t, y1), y2], axis=1)
    return first, last


def upright(x):
    return jnp.concatenate([x, jnp.zeros((64, 128), F32)], axis=0).T


REQ, DOC, ROWS, QUERY, DGRAD, PROB = range(6)
SIB_D, SIB_Q, SIB_H, SIB_G, SIB_DD, PART_Q, PART_DQ, PART_L = range(8)


def kernel(
    q_ref, d_ref, pool_ref, owner_ref, local_ref,
    loss_ref, dq_ref, dd_ref, gp_ref,
    idx_mine, idx_all, q_part, q_all, q_re, d_nat, d_sib, d_mine, d_raw, d_all, lr_all, sid,
    rq_out, rq_in, lt, pool_s,
    p_out, p_in, p_all, f_out, f_in, hs_mine, hs_sib, hq, st, ch, stat_out, stat_in,
    hc_out, hc_in, g3_out, g3_in, dd_out, dd_sib, dd_nat, g_sib_out, g_sib_in, g_out, g_in, wcat, at_s,
    dq_out, dq_in, loss_out, loss_in, lrow,
    plane_s, plane_r, row_s, row_r, idx_s, idx_r, qs, qr, gs, gr, one_s, one_r,
):
    blk, dim = lax.axis_index("blk"), lax.axis_index("dim")
    xy, z = blk // 8, blk % 8
    yh, c = dim // 2, dim % 2
    t = z // 2
    holder = (z % 2) == yh
    me_p = xy * 2 + yh
    me_r = z * 2 + c

    def plane_dev(p):
        return ((p // 2) * 8 + z, (p % 2) * 2 + c)

    def row_dev(r):
        return (xy * 8 + r // 2, yh * 2 + r % 2)

    def z_dev(zz):
        return (xy * 8 + zz, dim)

    sibling = (blk, yh * 2 + (1 - c))
    partner = (blk, (1 - yh) * 2 + c)

    def remote(src, dst, send, recv, device):
        return pltpu.make_async_remote_copy(
            src_ref=src, dst_ref=dst, send_sem=send, recv_sem=recv,
            device_id=device, device_id_type=MESH,
        )

    barrier = pltpu.get_barrier_semaphore()

    def greet(k):
        pl.semaphore_signal(barrier, inc=1, device_id=plane_dev((me_p + k + 1) % 16), device_id_type=MESH)
        pl.semaphore_signal(barrier, inc=1, device_id=row_dev((me_r + k + 1) % 16), device_id_type=MESH)

    loop(15, greet)
    idx_mine[0:8] = owner_ref[...]
    idx_mine[8:16] = local_ref[...]
    d_nat[...] = upright(d_ref[...])
    pl.semaphore_wait(barrier, 30)

    def idx_copy(zz):
        return remote(idx_mine, idx_all.at[t], idx_s.at[zz], idx_r.at[t], z_dev(zz))

    def q_copy(zz):
        return remote(q_all.at[c, t], q_all.at[c, t], qs.at[zz], qr.at[t], z_dev(zz))

    sib_d = remote(
        d_nat.at[pl.ds((1 - c) * 64, 64)], d_sib, one_s.at[SIB_D], one_r.at[SIB_D], sibling
    )
    part_q = remote(q_ref, q_part, one_s.at[PART_Q], one_r.at[PART_Q], partner)

    @pl.when(holder)
    def _():
        loop(7, lambda k: idx_copy((z + k + 1) % 8).start())
        idx_all[t] = idx_mine[...]

    sib_d.start()

    @pl.when(jnp.logical_not(holder))
    def _():
        part_q.start()

    for k, part in enumerate(split3(pool_ref[...])):
        pool_s[k, 0:192] = part
        pool_s[k, 192:256] = jnp.zeros((64, 2048), BF16)

    def idx_wait(tt):
        @pl.when(2 * tt + yh != z)
        def _():
            remote(idx_mine, idx_all.at[tt], idx_s.at[0], idx_r.at[tt], partner).wait_recv()

    loop(4, idx_wait)
    sub8 = lax.broadcasted_iota(jnp.int32, (8, 128), 0)
    upper = jnp.where(
        lax.broadcasted_iota(jnp.int32, (128, 128), 0) < lax.broadcasted_iota(jnp.int32, (128, 128), 1),
        1.0, 0.0,
    ).astype(BF16)
    for tt in range(4):
        owner = idx_all[tt, 0:8]
        local = idx_all[tt, 8:16] + 1
        table = jnp.zeros((8, 128), jnp.int32)
        for a in range(8):
            row = jnp.sum(jnp.where(owner == a * 8 + z, local, 0), axis=0, keepdims=True)
            table = jnp.where(sub8 == a, row, table)
        marks = jnp.where(table > 0, 1.0, 0.0)
        rank = mm(marks.astype(BF16), upper, NN)
        lr_all[:, tt * 128 : (tt + 1) * 128] = table.astype(F32)
        sid[:, tt * 128 : (tt + 1) * 128] = jnp.where(table > 0, rank + float(tt * 32), -1.0)

    sub512 = lax.broadcasted_iota(jnp.int32, (128, 512), 0).astype(F32)
    lane128 = lax.broadcasted_iota(jnp.int32, (128, 128), 1)

    def hot(a):
        return sub512 == sid[pl.ds(a, 1), :]

    def columns(rows):
        def step(a, table):
            col = jnp.sum(jnp.where(hot(a), rows[pl.ds(a, 1), :], 0.0), axis=1, keepdims=True)
            return jnp.where(lane128 == a, col, table)

        return lax.fori_loop(0, 8, step, jnp.zeros((128, 128), F32))

    wanted = columns(lr_all).T
    for a in range(8):
        rq_out[a] = wanted[a : a + 1, :]
    rq_in[me_p] = rq_out[xy]

    def req_copy(p, slot):
        return remote(
            rq_out.at[p // 2], rq_in.at[slot], plane_s.at[REQ, p], plane_r.at[REQ, slot], plane_dev(p)
        )

    loop(15, lambda k: req_copy((me_p + k + 1) % 16, me_p).start())

    @pl.when(holder)
    def _():
        remote(q_ref, q_part, one_s.at[PART_Q], one_r.at[PART_Q], partner).wait_recv()
        own, other = upright(q_ref[...]), upright(q_part[...])
        q_all[c, t] = fold(jnp.where(yh == 0, own, other), jnp.where(yh == 0, other, own))
        loop(7, lambda k: q_copy((z + k + 1) % 8).start())

    sib_d.wait_recv()
    own_d = d_nat[pl.ds(pl.multiple_of(c * 64, 64), 64), :]
    d_mine[...] = fold(jnp.where(c == 0, own_d, d_sib[...]), jnp.where(c == 0, d_sib[...], own_d))

    def doc_copy(p, slot):
        return remote(
            d_mine, d_raw.at[slot % 2, slot // 2],
            plane_s.at[DOC, p], plane_r.at[DOC, slot], plane_dev(p),
        )

    loop(15, lambda k: doc_copy((me_p + k + 1) % 16, me_p).start())
    d_raw[yh, xy] = d_mine[...]

    def req_wait(k):
        p = (me_p + k + 1) % 16
        req_copy(p, p).wait_recv()

    loop(15, req_wait)
    named = jnp.concatenate([rq_in[i] for i in range(16)] + [jnp.zeros((112, 128), F32)], axis=0)
    lt[...] = named.T
    lane2048 = lax.broadcasted_iota(jnp.int32, (128, 2048), 1).astype(F32) + 1.0

    def rows_copy(p, slot):
        return remote(
            p_out.at[p], p_in.at[slot % 2, slot // 2],
            plane_s.at[ROWS, p], plane_r.at[ROWS, slot], plane_dev(p),
        )

    def fetch(g):
        hots = []
        for i in range(4):
            col = jnp.sum(jnp.where(lane128 == g * 4 + i, lt[...], 0.0), axis=1, keepdims=True)
            hots.append(jnp.where(col == lane2048, 1.0, 0.0).astype(BF16))
        hots = jnp.concatenate(hots, axis=0)
        got = mm(hots, pool_s[0], NT) + mm(hots, pool_s[1], NT) + mm(hots, pool_s[2], NT)
        for i in range(4):
            p = g * 4 + i
            p_out[p] = fold(got[i * 128 : i * 128 + 64], got[i * 128 + 64 : i * 128 + 128])

            @pl.when(p != me_p)
            def _():
                rows_copy(p, me_p).start()

    loop(4, fetch)
    p_in[yh, xy] = p_out[me_p]

    def q_wait(tt):
        @pl.when(2 * tt + yh != z)
        def _():
            remote(q_all.at[c, tt], q_all.at[c, tt], qs.at[0], qr.at[tt], partner).wait_recv()

    loop(4, q_wait)
    sib_q = remote(q_all.at[c], q_all.at[c], one_s.at[SIB_Q], one_r.at[SIB_Q], sibling)
    sib_q.start()

    queries = split3(q_all[c].reshape(512, 384))

    def pick(g):
        hots = jnp.concatenate(
            [jnp.where(hot(g * 4 + i), 1.0, 0.0).astype(BF16) for i in range(4)], axis=0
        )
        got = mm(hots, queries[0], NN) + mm(hots, queries[1], NN) + mm(hots, queries[2], NN)
        for i in range(4):
            first, last = regroup(got[i * 128 : i * 128 + 64], got[i * 128 + 64 : i * 128 + 128])
            f_out[(g * 4 + i) * 2] = first
            f_out[(g * 4 + i) * 2 + 1] = last

    loop(2, pick)
    f_in[me_p] = f_out[me_p]

    remote(q_all.at[c], q_all.at[1 - c], one_s.at[SIB_Q], one_r.at[SIB_Q], sibling).wait_recv()

    def rearrange_q(tt):
        first, last = regroup(q_all[0, tt], q_all[1, tt])
        q_re[0, tt] = first
        q_re[1, tt] = last

    loop(4, rearrange_q)

    def doc_wait(k):
        p = (me_p + k + 1) % 16
        doc_copy(p, p).wait_recv()

    loop(15, doc_wait)

    def score(j):
        total = None
        for part in range(2):
            docs = d_raw[part, pl.ds(j * 4, 4)].reshape(256, 384)
            value = mm(docs, q_re[part].reshape(512, 384), NT, HIGHEST)
            total = value if total is None else total + value
        st[pl.ds(pl.multiple_of(j * 256, 256), 256), :] = total * SCALE

    loop(2, score)

    def top(j, best):
        rows = st[pl.ds(pl.multiple_of(j * 64, 64), 64), :].reshape(8, 8, 512)
        return jnp.maximum(best, jnp.max(rows, axis=0))

    best = lax.fori_loop(0, 8, top, jnp.full((8, 512), -jnp.inf, F32))
    best = jnp.max(best, axis=0, keepdims=True)

    def rows_wait(k):
        p = (me_p + k + 1) % 16
        rows_copy(p, p).wait_recv()

    loop(15, rows_wait)
    low64 = low(64)

    def hard_part(a, table):
        terms = p_in[0, a] * f_out[a * 2] + p_in[1, a] * f_out[a * 2 + 1]
        t0, t1, t2 = halves(terms)
        first = jnp.sum(t0 + jnp.where(low64, t1, 0.0), axis=1, keepdims=True)
        last = jnp.sum(t2 + jnp.where(low64, 0.0, t1), axis=1, keepdims=True)
        return jnp.where(lane128 == a, jnp.concatenate([first, last], axis=0), table)

    hs_mine[...] = lax.fori_loop(0, 8, hard_part, jnp.zeros((128, 128), F32))
    sib_h = remote(hs_mine, hs_sib, one_s.at[SIB_H], one_r.at[SIB_H], sibling)
    sib_h.start()

    def query_copy(p, slot):
        return remote(
            f_out.at[p], f_in.at[slot], plane_s.at[QUERY, p], plane_r.at[QUERY, slot], plane_dev(p)
        )

    loop(15, lambda k: query_copy((me_p + k + 1) % 16, me_p).start())

    sib_h.wait_recv()
    hard = (hs_mine[...] + hs_sib[...]) * SCALE
    for a in range(8):
        row = jnp.sum(jnp.where(hot(a), hard[:, a : a + 1], 0.0), axis=0, keepdims=True)
        hq[a : a + 1, :] = jnp.where(sid[a : a + 1, :] >= 0.0, row, -jnp.inf)
    peak = jnp.maximum(best, jnp.max(hq[...], axis=0, keepdims=True))

    def add(j, total):
        rows = jnp.exp(st[pl.ds(pl.multiple_of(j * 64, 64), 64), :] - peak)
        return total + jnp.sum(rows.reshape(8, 8, 512), axis=0)

    total = lax.fori_loop(0, 8, add, jnp.zeros((8, 512), F32))
    total = total + jnp.exp(hq[...] - peak) * jnp.where(c == 0, 1.0, 0.0)
    total = jnp.sum(total, axis=0, keepdims=True)
    square = st[pl.ds(pl.multiple_of(xy * 64, 64), 64), pl.ds(pl.multiple_of(t * 128, 128), 128)]
    on_diagonal = lax.broadcasted_iota(jnp.int32, (64, 128), 1) == (
        lax.broadcasted_iota(jnp.int32, (64, 128), 0) + c * 64
    )
    positive = jnp.sum(jnp.where(on_diagonal, square, 0.0), axis=0, keepdims=True)
    positive = positive * jnp.where(holder, 1.0, 0.0)
    positive = jnp.concatenate([positive] * 4, axis=1)
    here = lax.broadcasted_iota(jnp.int32, (1, 512), 1) // 128 == t
    positive = jnp.where(here, positive, 0.0)
    sub8w = lax.broadcasted_iota(jnp.int32, (8, 512), 0)
    stat_out[...] = jnp.where(sub8w == 0, peak, jnp.where(sub8w == 1, total, positive))
    stat_in[me_r] = stat_out[...]

    def stat_copy(r, slot):
        return remote(stat_out, stat_in.at[slot], row_s.at[r], row_r.at[slot], row_dev(r))

    loop(15, lambda k: stat_copy((me_r + k + 1) % 16, me_r).start())

    def rearrange_d(k):
        first, last = regroup(d_raw[0, k], d_raw[1, k])
        d_all[0, k] = first
        d_all[1, k] = last
        first, last = regroup(p_in[0, k], p_in[1, k])
        p_all[k, 0:64] = first
        p_all[k, 64:128] = last

    loop(8, rearrange_d)
    filler = jnp.zeros((120, 512), F32)
    sid_t = jnp.concatenate([sid[...], filler], axis=0).T

    def stat_wait(k):
        r = (me_r + k + 1) % 16
        stat_copy(r, r).wait_recv()

    loop(15, stat_wait)
    peak = stat_in[0, 0:1, :]
    for r in range(1, 16):
        peak = jnp.maximum(peak, stat_in[r, 0:1, :])
    total = jnp.zeros((1, 512), F32)
    positive = jnp.zeros((1, 512), F32)
    for r in range(16):
        total = total + stat_in[r, 1:2, :] * jnp.exp(stat_in[r, 0:1, :] - peak)
        positive = positive + stat_in[r, 2:3, :]
    log_total = peak + jnp.log(total)
    lrow[...] = log_total - positive

    hq[...] = jnp.exp(hq[...] - log_total)

    def chance(j):
        rows = pl.ds(pl.multiple_of(j * 128, 128), 128)
        value = jnp.exp(st[rows, :] - log_total)
        st[rows, :] = value
        ch[:, rows] = value.T

    loop(4, chance)

    g_sib_out[...] = mm(ch[...], d_all[1 - c].reshape(512, 384), NN, HIGHEST)
    sib_g = remote(g_sib_out, g_sib_in, one_s.at[SIB_G], one_r.at[SIB_G], sibling)
    sib_g.start()
    hc_t = jnp.concatenate([hq[...], filler], axis=0).T
    lane512 = lax.broadcasted_iota(jnp.int32, (512, 128), 1).astype(F32)
    for a in range(8):
        wcat[:, a * 128 : (a + 1) * 128] = jnp.where(
            sid_t[:, a : a + 1] == lane512, hc_t[:, a : a + 1], 0.0
        )
    g_own = mm(ch[...], d_all[c].reshape(512, 384), NN, HIGHEST)
    g_own = g_own + mm(wcat[...], p_all[...].reshape(1024, 384), NN, HIGHEST)
    sib_g.wait_recv()
    g_out[...] = (g_own + g_sib_in[...]).reshape(4, 128, 384)

    def grad_copy(tt, slot):
        return remote(g_out.at[tt], g_in.at[slot], gs.at[tt], gr.at[slot], z_dev(2 * tt + yh))

    def grad_send(tt):
        @pl.when(2 * tt + yh != z)
        def _():
            grad_copy(tt, z).start()

    loop(4, grad_send)

    @pl.when(holder)
    def _():
        g_in[z] = g_out[t]

    def doc_grad(part):
        value = mm(st[...], q_re[part].reshape(512, 384), NN, HIGHEST)
        g3_out[:, part] = value.reshape(8, 64, 384)

    loop(2, doc_grad)

    def dgrad_copy(p, slot):
        return remote(
            g3_out.at[p // 2, p % 2], g3_in.at[slot],
            plane_s.at[DGRAD, p], plane_r.at[DGRAD, slot], plane_dev(p),
        )

    chances = columns(hq).T
    for a in range(8):
        hc_out[a] = chances[a : a + 1, :]
    hc_in[me_p] = hc_out[xy]

    def prob_copy(p, slot):
        return remote(
            hc_out.at[p // 2], hc_in.at[slot], plane_s.at[PROB, p], plane_r.at[PROB, slot], plane_dev(p)
        )

    loop(15, lambda k: prob_copy((me_p + k + 1) % 16, me_p).start())
    loop(15, lambda k: dgrad_copy((me_p + k + 1) % 16, me_p).start())
    g3_in[me_p] = g3_out[xy, yh]

    def query_wait(k):
        p = (me_p + k + 1) % 16
        query_copy(p, p).wait_recv()
        prob_copy(p, p).wait_recv()

    loop(15, query_wait)
    chances = jnp.concatenate([hc_in[i] for i in range(16)] + [jnp.zeros((112, 128), F32)], axis=0).T

    def turn(i):
        col = jnp.sum(jnp.where(lane128 == i, chances, 0.0), axis=1, keepdims=True)
        rows = jnp.concatenate(unfold(f_in[i]), axis=0) * (col * SCALE)
        terms = split3(rows.T[0:192])
        for k in range(3):
            at_s[k, :, pl.ds(pl.multiple_of(i * 128, 128), 128)] = terms[k]

    loop(16, turn)
    lane256 = lax.broadcasted_iota(jnp.int32, (128, 256), 1).astype(F32) + 1.0

    def pool_grad(n):
        base = (n * 256).astype(F32)
        hots = jnp.concatenate(
            [
                jnp.where(lt[:, i : i + 1] == lane256 + base, 1.0, 0.0).astype(BF16)
                for i in range(16)
            ],
            axis=0,
        )
        value = mm(at_s[0], hots, NN) + mm(at_s[1], hots, NN) + mm(at_s[2], hots, NN)
        gp_ref[:, pl.ds(pl.multiple_of(n * 256, 256), 256)] = value

    loop(8, pool_grad)

    part_dq = remote(dq_out, dq_in, one_s.at[PART_DQ], one_r.at[PART_DQ], partner)
    part_l = remote(loss_out, loss_in, one_s.at[PART_L], one_r.at[PART_L], partner)

    @pl.when(holder)
    def _():
        loss_out[...] = lrow[:, pl.ds(pl.multiple_of(t * 128, 128), 128)]
        part_l.start()

        def wait(k):
            zz = (z + k + 1) % 8
            grad_copy(t, zz).wait_recv()

        loop(7, wait)
        value = g_in[0]
        for zz in range(1, 8):
            value = value + g_in[zz]
        first, last = unfold(value)
        dq_out[...] = jnp.where(yh == 0, last, first).T[0:192]
        part_dq.start()
        dq_ref[...] = (jnp.where(yh == 0, first, last).T[0:192] - d_ref[...]) * SCALE
        loss_ref[...] = loss_out[...]

    def dgrad_wait(k):
        p = (me_p + k + 1) % 16
        dgrad_copy(p, p).wait_recv()

    loop(15, dgrad_wait)
    value = g3_in[0]
    for p in range(1, 16):
        value = value + g3_in[p]
    first, last = unfold(value)
    dd_out[...] = jnp.where(c == 0, last, first)
    sib_dd = remote(dd_out, dd_sib, one_s.at[SIB_DD], one_r.at[SIB_DD], sibling)
    sib_dd.start()
    dd_nat[pl.ds(pl.multiple_of(c * 64, 64), 64), :] = jnp.where(c == 0, first, last)

    @pl.when(jnp.logical_not(holder))
    def _():
        part_l.wait_recv()
        loss_ref[...] = loss_in[...]
        part_dq.wait_recv()
        dq_ref[...] = (dq_in[...] - d_ref[...]) * SCALE

    sib_dd.wait_recv()
    dd_nat[pl.ds(pl.multiple_of((1 - c) * 64, 64), 64), :] = dd_sib[...]
    dd_ref[...] = (dd_nat[...].T[0:192] - q_ref[...]) * SCALE

    sib_d.wait_send()
    sib_q.wait_send()
    sib_h.wait_send()
    sib_g.wait_send()
    sib_dd.wait_send()

    def sent(k):
        p = (me_p + k + 1) % 16
        for copy in (doc_copy, req_copy, rows_copy, query_copy, prob_copy, dgrad_copy):
            copy(p, me_p).wait_send()
        stat_copy((me_r + k + 1) % 16, me_r).wait_send()

    loop(15, sent)

    def grad_sent(tt):
        @pl.when(2 * tt + yh != z)
        def _():
            grad_copy(tt, z).wait_send()

    loop(4, grad_sent)

    @pl.when(holder)
    def _():
        def z_sent(k):
            zz = (z + k + 1) % 8
            idx_copy(zz).wait_send()
            q_copy(zz).wait_send()

        loop(7, z_sent)
        part_l.wait_send()
        part_dq.wait_send()

    @pl.when(jnp.logical_not(holder))
    def _():
        part_q.wait_send()


def per_device(question_matrix, document_matrix, pool, hard_owner, hard_local):
    vmem = pl.BlockSpec(memory_space=pltpu.VMEM)
    f = lambda *shape: pltpu.VMEM(shape, F32)
    scratch = [
        pltpu.VMEM((16, 128), jnp.int32),
        pltpu.VMEM((4, 16, 128), jnp.int32),
        f(192, 128),
        f(2, 4, 128, 384),
        f(2, 4, 128, 384),
        f(128, 256),
        f(64, 256),
        f(64, 384),
        f(2, 8, 64, 384),
        f(2, 8, 64, 384),
        f(8, 512),
        f(8, 512),
        f(8, 1, 128),
        f(16, 1, 128),
        f(128, 128),
        pltpu.VMEM((3, 256, 2048), BF16),
        f(16, 64, 384),
        f(2, 8, 64, 384),
        f(8, 128, 384),
        f(16, 64, 384),
        f(16, 64, 384),
        f(128, 128),
        f(128, 128),
        f(8, 512),
        f(512, 512),
        f(512, 512),
        f(8, 512),
        f(16, 8, 512),
        f(8, 1, 128),
        f(16, 1, 128),
        f(8, 2, 64, 384),
        f(16, 64, 384),
        f(64, 256),
        f(64, 256),
        f(128, 256),
        f(512, 384),
        f(512, 384),
        f(4, 128, 384),
        f(8, 128, 384),
        f(512, 1024),
        pltpu.VMEM((3, 192, 2048), BF16),
        f(192, 128),
        f(192, 128),
        f(1, 128),
        f(1, 128),
        f(1, 512),
        pltpu.SemaphoreType.DMA((6, 16)),
        pltpu.SemaphoreType.DMA((6, 16)),
        pltpu.SemaphoreType.DMA((16,)),
        pltpu.SemaphoreType.DMA((16,)),
        pltpu.SemaphoreType.DMA((8,)),
        pltpu.SemaphoreType.DMA((4,)),
        pltpu.SemaphoreType.DMA((8,)),
        pltpu.SemaphoreType.DMA((4,)),
        pltpu.SemaphoreType.DMA((4,)),
        pltpu.SemaphoreType.DMA((8,)),
        pltpu.SemaphoreType.DMA((8,)),
        pltpu.SemaphoreType.DMA((8,)),
    ]
    loss, dq, dd, gp = pl.pallas_call(
        kernel,
        name="retriever_step",
        out_shape=(
            jax.ShapeDtypeStruct((1, 128), F32),
            jax.ShapeDtypeStruct((192, 128), F32),
            jax.ShapeDtypeStruct((192, 128), F32),
            jax.ShapeDtypeStruct((192, 2048), F32),
        ),
        in_specs=[vmem] * 5,
        out_specs=(vmem,) * 4,
        scratch_shapes=scratch,
        compiler_params=pltpu.CompilerParams(
            collective_id=0, has_side_effects=True, vmem_limit_bytes=60 * 1024 * 1024
        ),
    )(question_matrix.T, document_matrix.T, pool, hard_owner.T, hard_local.T)
    return loss.reshape(128), dq.T, dd.T, gp


def solution(mesh):
    placed = (P("blk", "dim"), P("blk", "dim"), P("dim", "blk"), P("blk", None), P("blk", None))
    return jax.shard_map(
        per_device,
        mesh=mesh,
        in_specs=placed,
        out_specs=(P("blk"), P("blk", "dim"), P("blk", "dim"), P("dim", "blk")),
        check_vma=False,
    )
```

time: 182 us -> 134 us (0.74)
  the two profiles are of different devices: /device:TPU:84 before, /device:TPU:16 now
where the time goes in v2:
time: 134 us; the launch traced here: 132 us
  Pallas kernels  124 us (93%)
  local copies, waits for them, and re-layouts  6.93 us (5%)
    pallas_call x1, Pallas kernels, per_device(): pl.pallas_call(kernel, name='retriever_step', out_shape=(jax.ShapeDtypeSt...  124 us
    unnamed x4, local copies, waits for them, and re-layouts  6.93 us

profile of v2, /device:TPU:16, one launch (start us, length us, event | category | flops | bytes accessed | tf_op | source)
XLA Modules:
  0.0 131.8 jit_solution(7936361359430417588)
XLA Ops:
  0.6 124.3 %retriever_step.1 = (f32[1,128]{1,0:T(1,128)}, f32[192,128]{1,0:T(8,128)}, f32[192,128]{1,0:T(8,128)}, f32[192,2048]{1,0:T(8,128)}) custom-call(f32[192,128]{1,0:T(8,128)} %bitcast.7, f32[192,128]{1,0:T(8,128)} %bitcast.8, f32[192,2048]{1,0:T(8,128)} %pool_ref.1, s32[8,128]{1,0:T(8,128)} %bitcast.11, s32[8,128]{1,0:T(8,128)} %bitcast.12), custom_call_target="tpu_custom_call" | custom-call | tf_op jit(solution)/shard_map/retriever_step/pallas_call | solution.py:644
  124.9 1.1 copy.13
  126.1 1.5 %copy.14 = f32[128,192]{0,1:T(8,128)} copy(f32[128,192]{0,1:T(8,128)} %bitcast.10) | data formatting | bytes 196608
  127.6 1.5 %copy.15 = f32[128,192]{0,1:T(8,128)} copy(f32[128,192]{0,1:T(8,128)} %bitcast.9) | data formatting | bytes 196608
  129.1 2.7 %copy.16 = f32[192,2048]{1,0:T(8,128)} copy(f32[192,2048]{1,0:T(8,128)} %get-tuple-element.19) | data formatting | bytes 3145728

commit v3 on v2

--- a/solution.py
+++ b/solution.py
@@ -78,19 +78,20 @@
     return jnp.concatenate([x, jnp.zeros((64, 128), F32)], axis=0).T
 
 
-REQ, DOC, ROWS, QUERY, DGRAD, PROB = range(6)
-SIB_D, SIB_Q, SIB_H, SIB_G, SIB_DD, PART_Q, PART_DQ, PART_L = range(8)
+REQ, ROWS, QUERY, PROB = range(4)
+SIB_D, SIB_Q, SIB_H, SIB_G, SIB_DD, SIB_P, PART_Q, PART_DQ, PART_L = range(9)
+DOC_1, DOC_2, GRAD_1, GRAD_2 = range(4)
 
 
 def kernel(
     q_ref, d_ref, pool_ref, owner_ref, local_ref,
     loss_ref, dq_ref, dd_ref, gp_ref,
-    idx_mine, idx_all, q_part, q_all, q_re, d_nat, d_sib, d_mine, d_raw, d_all, lr_all, sid,
+    idx_mine, idx_all, q_part, q_all, q_re, d_nat, d_sib, d_raw, d_all, lr_all, sid,
     rq_out, rq_in, lt, pool_s,
     p_out, p_in, p_all, f_out, f_in, hs_mine, hs_sib, hq, st, ch, stat_out, stat_in,
-    hc_out, hc_in, g3_out, g3_in, dd_out, dd_sib, dd_nat, g_sib_out, g_sib_in, g_out, g_in, wcat, at_s,
-    dq_out, dq_in, loss_out, loss_in, lrow,
-    plane_s, plane_r, row_s, row_r, idx_s, idx_r, qs, qr, gs, gr, one_s, one_r,
+    hc_out, hc_in, g3_out, c1x, c1y, cx, cy, c2x, c2y, dd_out, dd_sib, dd_nat, g_sib_out, g_sib_in, g_out, g_in, wcat, at_s,
+    dq_out, dq_in, loss_out, loss_in, pos_out, pos_in, lrow,
+    plane_s, plane_r, x_s, x_r, y_s, y_r, row_s, row_r, idx_s, idx_r, qs, qr, gs, gr, one_s, one_r,
 ):
     blk, dim = lax.axis_index("blk"), lax.axis_index("dim")
     xy, z = blk // 8, blk % 8
@@ -99,12 +100,20 @@
     holder = (z % 2) == yh
     me_p = xy * 2 + yh
     me_r = z * 2 + c
+    x, yl = xy // 2, xy % 2
+    y = yh * 2 + yl
 
     def plane_dev(p):
         return ((p // 2) * 8 + z, (p % 2) * 2 + c)
 
     def row_dev(r):
         return (xy * 8 + r // 2, yh * 2 + r % 2)
+
+    def x_dev(xx):
+        return ((xx * 2 + yl) * 8 + z, dim)
+
+    def y_dev(yy):
+        return ((x * 2 + yy % 2) * 8 + z, (yy // 2) * 2 + c)
 
     def z_dev(zz):
         return (xy * 8 + zz, dim)
@@ -128,6 +137,9 @@
     idx_mine[0:8] = owner_ref[...]
     idx_mine[8:16] = local_ref[...]
     d_nat[...] = upright(d_ref[...])
+    for k, part in enumerate(split3(pool_ref[...])):
+        pool_s[k, 0:192] = part
+        pool_s[k, 192:256] = jnp.zeros((64, 2048), BF16)
     pl.semaphore_wait(barrier, 30)
 
     def idx_copy(zz):
@@ -152,9 +164,40 @@
     def _():
         part_q.start()
 
-    for k, part in enumerate(split3(pool_ref[...])):
-        pool_s[k, 0:192] = part
-        pool_s[k, 192:256] = jnp.zeros((64, 2048), BF16)
+    sib_d.wait_recv()
+    own_d = d_nat[pl.ds(pl.multiple_of(c * 64, 64), 64), :]
+    d_raw[yh, x, yl] = fold(
+        jnp.where(c == 0, own_d, d_sib[...]), jnp.where(c == 0, d_sib[...], own_d)
+    )
+
+    def doc_x1(xx, slot):
+        piece = d_raw.at[yh, slot, yl, pl.ds(0, 32)]
+        return remote(piece, piece, x_s.at[DOC_1, xx], x_r.at[DOC_1, slot], x_dev(xx))
+
+    def doc_y1(yy, slot):
+        piece = d_raw.at[slot // 2, x, slot % 2, pl.ds(32, 32)]
+        return remote(piece, piece, y_s.at[DOC_1, yy], y_r.at[DOC_1, slot], y_dev(yy))
+
+    def doc_y2(yy, slot):
+        piece = d_raw.at[slot // 2, :, slot % 2, pl.ds(0, 32)]
+        return remote(piece, piece, y_s.at[DOC_2, yy], y_r.at[DOC_2, slot], y_dev(yy))
+
+    def doc_x2(xx, slot):
+        piece = d_raw.at[:, slot, :, pl.ds(32, 32)]
+        return remote(piece, piece, x_s.at[DOC_2, xx], x_r.at[DOC_2, slot], x_dev(xx))
+
+    def doc_first(k):
+        doc_x1((x + k + 1) % 4, x).start()
+        doc_y1((y + k + 1) % 4, y).start()
+
+    loop(3, doc_first)
+
+    @pl.when(holder)
+    def _():
+        remote(q_ref, q_part, one_s.at[PART_Q], one_r.at[PART_Q], partner).wait_recv()
+        own, other = upright(q_ref[...]), upright(q_part[...])
+        q_all[c, t] = fold(jnp.where(yh == 0, own, other), jnp.where(yh == 0, other, own))
+        loop(7, lambda k: q_copy((z + k + 1) % 8).start())
 
     def idx_wait(tt):
         @pl.when(2 * tt + yh != z)
@@ -204,25 +247,18 @@
 
     loop(15, lambda k: req_copy((me_p + k + 1) % 16, me_p).start())
 
-    @pl.when(holder)
-    def _():
-        remote(q_ref, q_part, one_s.at[PART_Q], one_r.at[PART_Q], partner).wait_recv()
-        own, other = upright(q_ref[...]), upright(q_part[...])
-        q_all[c, t] = fold(jnp.where(yh == 0, own, other), jnp.where(yh == 0, other, own))
-        loop(7, lambda k: q_copy((z + k + 1) % 8).start())
-
-    sib_d.wait_recv()
-    own_d = d_nat[pl.ds(pl.multiple_of(c * 64, 64), 64), :]
-    d_mine[...] = fold(jnp.where(c == 0, own_d, d_sib[...]), jnp.where(c == 0, d_sib[...], own_d))
-
-    def doc_copy(p, slot):
-        return remote(
-            d_mine, d_raw.at[slot % 2, slot // 2],
-            plane_s.at[DOC, p], plane_r.at[DOC, slot], plane_dev(p),
-        )
-
-    loop(15, lambda k: doc_copy((me_p + k + 1) % 16, me_p).start())
-    d_raw[yh, xy] = d_mine[...]
+    def doc_second(k):
+        xx, yy = (x + k + 1) % 4, (y + k + 1) % 4
+        doc_x1(xx, xx).wait_recv()
+        doc_y1(yy, yy).wait_recv()
+
+    loop(3, doc_second)
+
+    def doc_on(k):
+        doc_y2((y + k + 1) % 4, y).start()
+        doc_x2((x + k + 1) % 4, x).start()
+
+    loop(3, doc_on)
 
     def req_wait(k):
         p = (me_p + k + 1) % 16
@@ -291,15 +327,16 @@
     loop(4, rearrange_q)
 
     def doc_wait(k):
-        p = (me_p + k + 1) % 16
-        doc_copy(p, p).wait_recv()
-
-    loop(15, doc_wait)
+        xx, yy = (x + k + 1) % 4, (y + k + 1) % 4
+        doc_y2(yy, yy).wait_recv()
+        doc_x2(xx, xx).wait_recv()
+
+    loop(3, doc_wait)
 
     def score(j):
         total = None
         for part in range(2):
-            docs = d_raw[part, pl.ds(j * 4, 4)].reshape(256, 384)
+            docs = d_raw[part, pl.ds(j * 2, 2)].reshape(256, 384)
             value = mm(docs, q_re[part].reshape(512, 384), NT, HIGHEST)
             total = value if total is None else total + value
         st[pl.ds(pl.multiple_of(j * 256, 256), 256), :] = total * SCALE
@@ -357,21 +394,20 @@
         lax.broadcasted_iota(jnp.int32, (64, 128), 0) + c * 64
     )
     positive = jnp.sum(jnp.where(on_diagonal, square, 0.0), axis=0, keepdims=True)
-    positive = positive * jnp.where(holder, 1.0, 0.0)
-    positive = jnp.concatenate([positive] * 4, axis=1)
-    here = lax.broadcasted_iota(jnp.int32, (1, 512), 1) // 128 == t
-    positive = jnp.where(here, positive, 0.0)
-    sub8w = lax.broadcasted_iota(jnp.int32, (8, 512), 0)
-    stat_out[...] = jnp.where(sub8w == 0, peak, jnp.where(sub8w == 1, total, positive))
+    pos_out[...] = positive
+    sib_p = remote(pos_out, pos_in, one_s.at[SIB_P], one_r.at[SIB_P], sibling)
+    stat_out[:, 0:512] = peak
+    stat_out[:, 512:1024] = total
     stat_in[me_r] = stat_out[...]
 
     def stat_copy(r, slot):
         return remote(stat_out, stat_in.at[slot], row_s.at[r], row_r.at[slot], row_dev(r))
 
     loop(15, lambda k: stat_copy((me_r + k + 1) % 16, me_r).start())
+    sib_p.start()
 
     def rearrange_d(k):
-        first, last = regroup(d_raw[0, k], d_raw[1, k])
+        first, last = regroup(d_raw[0, k // 2, k % 2], d_raw[1, k // 2, k % 2])
         d_all[0, k] = first
         d_all[1, k] = last
         first, last = regroup(p_in[0, k], p_in[1, k])
@@ -387,16 +423,12 @@
         stat_copy(r, r).wait_recv()
 
     loop(15, stat_wait)
-    peak = stat_in[0, 0:1, :]
-    for r in range(1, 16):
-        peak = jnp.maximum(peak, stat_in[r, 0:1, :])
-    total = jnp.zeros((1, 512), F32)
-    positive = jnp.zeros((1, 512), F32)
-    for r in range(16):
-        total = total + stat_in[r, 1:2, :] * jnp.exp(stat_in[r, 0:1, :] - peak)
-        positive = positive + stat_in[r, 2:3, :]
+    peaks = jnp.concatenate([stat_in[r, :, 0:512] for r in range(16)], axis=0)
+    totals = jnp.concatenate([stat_in[r, :, 512:1024] for r in range(16)], axis=0)
+    peak = jnp.max(peaks, axis=0, keepdims=True)
+    total = jnp.sum(totals * jnp.exp(peaks - peak), axis=0, keepdims=True)
     log_total = peak + jnp.log(total)
-    lrow[...] = log_total - positive
+    lrow[...] = log_total
 
     hq[...] = jnp.exp(hq[...] - log_total)
 
@@ -438,16 +470,35 @@
 
     def doc_grad(part):
         value = mm(st[...], q_re[part].reshape(512, 384), NN, HIGHEST)
-        g3_out[:, part] = value.reshape(8, 64, 384)
+        g3_out[part] = value.reshape(4, 2, 64, 384)
 
     loop(2, doc_grad)
 
-    def dgrad_copy(p, slot):
+    def grad_y1(yy, slot):
         return remote(
-            g3_out.at[p // 2, p % 2], g3_in.at[slot],
-            plane_s.at[DGRAD, p], plane_r.at[DGRAD, slot], plane_dev(p),
-        )
-
+            g3_out.at[yy // 2, :, yy % 2, pl.ds(0, 32)], c1y.at[slot],
+            y_s.at[GRAD_1, yy], y_r.at[GRAD_1, slot], y_dev(yy),
+        )
+
+    def grad_x1(xx, slot):
+        return remote(
+            g3_out.at[:, xx, :, pl.ds(32, 32)], c1x.at[slot],
+            x_s.at[GRAD_1, xx], x_r.at[GRAD_1, slot], x_dev(xx),
+        )
+
+    def grad_x2(xx, slot):
+        return remote(cy.at[xx], c2x.at[slot], x_s.at[GRAD_2, xx], x_r.at[GRAD_2, slot], x_dev(xx))
+
+    def grad_y2(yy, slot):
+        return remote(
+            cx.at[yy // 2, yy % 2], c2y.at[slot], y_s.at[GRAD_2, yy], y_r.at[GRAD_2, slot], y_dev(yy)
+        )
+
+    def grad_first(k):
+        grad_y1((y + k + 1) % 4, y).start()
+        grad_x1((x + k + 1) % 4, x).start()
+
+    loop(3, grad_first)
     chances = columns(hq).T
     for a in range(8):
         hc_out[a] = chances[a : a + 1, :]
@@ -459,8 +510,6 @@
         )
 
     loop(15, lambda k: prob_copy((me_p + k + 1) % 16, me_p).start())
-    loop(15, lambda k: dgrad_copy((me_p + k + 1) % 16, me_p).start())
-    g3_in[me_p] = g3_out[xy, yh]
 
     def query_wait(k):
         p = (me_p + k + 1) % 16
@@ -474,7 +523,7 @@
         col = jnp.sum(jnp.where(lane128 == i, chances, 0.0), axis=1, keepdims=True)
         rows = jnp.concatenate(unfold(f_in[i]), axis=0) * (col * SCALE)
         terms = split3(rows.T[0:192])
-        for k in range(3):
+        for k in range(2):
             at_s[k, :, pl.ds(pl.multiple_of(i * 128, 128), 128)] = terms[k]
 
     loop(16, turn)
@@ -489,17 +538,47 @@
             ],
             axis=0,
         )
-        value = mm(at_s[0], hots, NN) + mm(at_s[1], hots, NN) + mm(at_s[2], hots, NN)
+        value = mm(at_s[0], hots, NN) + mm(at_s[1], hots, NN)
         gp_ref[:, pl.ds(pl.multiple_of(n * 256, 256), 256)] = value
 
-    loop(8, pool_grad)
+    loop(4, pool_grad)
+
+    def grad_second(k):
+        xx, yy = (x + k + 1) % 4, (y + k + 1) % 4
+        grad_y1(yy, yy).wait_recv()
+        grad_x1(xx, xx).wait_recv()
+
+    loop(3, grad_second)
+
+    def sum_y(xx):
+        cy[xx] = (g3_out[yh, xx, yl, 0:32] + c1y[(y + 1) % 4, xx]) + (
+            c1y[(y + 2) % 4, xx] + c1y[(y + 3) % 4, xx]
+        )
+
+    loop(4, sum_y)
+
+    def sum_x(k):
+        a, b = k // 2, k % 2
+        cx[a, b] = (g3_out[a, x, b, 32:64] + c1x[(x + 1) % 4, a, b]) + (
+            c1x[(x + 2) % 4, a, b] + c1x[(x + 3) % 4, a, b]
+        )
+
+    loop(4, sum_x)
+
+    def grad_on(k):
+        grad_x2((x + k + 1) % 4, x).start()
+        grad_y2((y + k + 1) % 4, y).start()
+
+    loop(3, grad_on)
+    loop(4, lambda n: pool_grad(n + 4))
 
     part_dq = remote(dq_out, dq_in, one_s.at[PART_DQ], one_r.at[PART_DQ], partner)
     part_l = remote(loss_out, loss_in, one_s.at[PART_L], one_r.at[PART_L], partner)
+    sib_p.wait_recv()
 
     @pl.when(holder)
     def _():
-        loss_out[...] = lrow[:, pl.ds(pl.multiple_of(t * 128, 128), 128)]
+        loss_out[...] = lrow[:, pl.ds(pl.multiple_of(t * 128, 128), 128)] - (pos_out[...] + pos_in[...])
         part_l.start()
 
         def wait(k):
@@ -516,14 +595,15 @@
         dq_ref[...] = (jnp.where(yh == 0, first, last).T[0:192] - d_ref[...]) * SCALE
         loss_ref[...] = loss_out[...]
 
-    def dgrad_wait(k):
-        p = (me_p + k + 1) % 16
-        dgrad_copy(p, p).wait_recv()
-
-    loop(15, dgrad_wait)
-    value = g3_in[0]
-    for p in range(1, 16):
-        value = value + g3_in[p]
+    def grad_wait(k):
+        xx, yy = (x + k + 1) % 4, (y + k + 1) % 4
+        grad_x2(xx, xx).wait_recv()
+        grad_y2(yy, yy).wait_recv()
+
+    loop(3, grad_wait)
+    upper_rows = (cy[x] + c2x[(x + 1) % 4]) + (c2x[(x + 2) % 4] + c2x[(x + 3) % 4])
+    lower_rows = (cx[yh, yl] + c2y[(y + 1) % 4]) + (c2y[(y + 2) % 4] + c2y[(y + 3) % 4])
+    value = jnp.concatenate([upper_rows, lower_rows], axis=0)
     first, last = unfold(value)
     dd_out[...] = jnp.where(c == 0, last, first)
     sib_dd = remote(dd_out, dd_sib, one_s.at[SIB_DD], one_r.at[SIB_DD], sibling)
@@ -549,11 +629,20 @@
 
     def sent(k):
         p = (me_p + k + 1) % 16
-        for copy in (doc_copy, req_copy, rows_copy, query_copy, prob_copy, dgrad_copy):
+        for copy in (req_copy, rows_copy, query_copy, prob_copy):
             copy(p, me_p).wait_send()
         stat_copy((me_r + k + 1) % 16, me_r).wait_send()
 
     loop(15, sent)
+
+    def sent4(k):
+        for copy in (doc_x1, doc_x2, grad_x1, grad_x2):
+            copy((x + k + 1) % 4, x).wait_send()
+        for copy in (doc_y1, doc_y2, grad_y1, grad_y2):
+            copy((y + k + 1) % 4, y).wait_send()
+
+    loop(3, sent4)
+    sib_p.wait_send()
 
     def grad_sent(tt):
         @pl.when(2 * tt + yh != z)
@@ -576,6 +665,11 @@
     @pl.when(jnp.logical_not(holder))
     def _():
         part_q.wait_send()
+
+
+def hand_on(*refs):
+    for source, target in zip(refs[:4], refs[4:]):
+        target[...] = source[...]
 
 
 def per_device(question_matrix, document_matrix, pool, hard_owner, hard_local):
@@ -589,8 +683,7 @@
         f(2, 4, 128, 384),
         f(128, 256),
         f(64, 256),
-        f(64, 384),
-        f(2, 8, 64, 384),
+        f(2, 4, 2, 64, 384),
         f(2, 8, 64, 384),
         f(8, 512),
         f(8, 512),
@@ -608,12 +701,17 @@
         f(8, 512),
         f(512, 512),
         f(512, 512),
-        f(8, 512),
-        f(16, 8, 512),
+        f(1, 1024),
+        f(16, 1, 1024),
         f(8, 1, 128),
         f(16, 1, 128),
-        f(8, 2, 64, 384),
-        f(16, 64, 384),
+        f(2, 4, 2, 64, 384),
+        f(4, 2, 2, 32, 384),
+        f(4, 4, 32, 384),
+        f(2, 2, 32, 384),
+        f(4, 32, 384),
+        f(4, 32, 384),
+        f(4, 32, 384),
         f(64, 256),
         f(64, 256),
         f(128, 256),
@@ -622,14 +720,20 @@
         f(4, 128, 384),
         f(8, 128, 384),
         f(512, 1024),
-        pltpu.VMEM((3, 192, 2048), BF16),
+        pltpu.VMEM((2, 192, 2048), BF16),
         f(192, 128),
         f(192, 128),
         f(1, 128),
         f(1, 128),
+        f(1, 128),
+        f(1, 128),
         f(1, 512),
-        pltpu.SemaphoreType.DMA((6, 16)),
-        pltpu.SemaphoreType.DMA((6, 16)),
+        pltpu.SemaphoreType.DMA((4, 16)),
+        pltpu.SemaphoreType.DMA((4, 16)),
+        pltpu.SemaphoreType.DMA((4, 4)),
+        pltpu.SemaphoreType.DMA((4, 4)),
+        pltpu.SemaphoreType.DMA((4, 4)),
+        pltpu.SemaphoreType.DMA((4, 4)),
         pltpu.SemaphoreType.DMA((16,)),
         pltpu.SemaphoreType.DMA((16,)),
         pltpu.SemaphoreType.DMA((8,)),
@@ -638,10 +742,10 @@
         pltpu.SemaphoreType.DMA((4,)),
         pltpu.SemaphoreType.DMA((4,)),
         pltpu.SemaphoreType.DMA((8,)),
-        pltpu.SemaphoreType.DMA((8,)),
-        pltpu.SemaphoreType.DMA((8,)),
+        pltpu.SemaphoreType.DMA((9,)),
+        pltpu.SemaphoreType.DMA((9,)),
     ]
-    loss, dq, dd, gp = pl.pallas_call(
+    results = pl.pallas_call(
         kernel,
         name="retriever_step",
         out_shape=(
@@ -657,6 +761,13 @@
             collective_id=0, has_side_effects=True, vmem_limit_bytes=60 * 1024 * 1024
         ),
     )(question_matrix.T, document_matrix.T, pool, hard_owner.T, hard_local.T)
+    loss, dq, dd, gp = pl.pallas_call(
+        hand_on,
+        name="results",
+        out_shape=tuple(jax.ShapeDtypeStruct(r.shape, r.dtype) for r in results),
+        in_specs=[vmem] * 4,
+        out_specs=(vmem,) * 4,
+    )(*results)
     return loss.reshape(128), dq.T, dd.T, gp
 
 

time: 134 us -> 109 us (0.81)
  the two profiles are of different devices: /device:TPU:16 before, /device:TPU:1 now
where the time goes in v3:
time: 109 us; the launch traced here: 108 us
  Pallas kernels  108 us (99%)
    pallas_call x1, Pallas kernels, per_device(): pl.pallas_call(kernel, name='retriever_step', out_shape=(jax.ShapeDtypeSt...  105 us
    pallas_call x1, Pallas kernels, per_device(): pl.pallas_call(hand_on, name='results', out_shape=tuple((jax.ShapeDtypeSt...  2.79 us

profile of v3, /device:TPU:1, one launch (start us, length us, event | category | flops | bytes accessed | tf_op | source)
XLA Modules:
  0.0 108.4 jit_solution(16422129994551263920)
XLA Ops:
  0.6 105.0 %retriever_step.1 = (f32[1,128]{1,0:T(1,128)}, f32[192,128]{1,0:T(8,128)}, f32[192,128]{1,0:T(8,128)}, f32[192,2048]{1,0:T(8,128)}) custom-call(f32[192,128]{1,0:T(8,128)} %bitcast.7, f32[192,128]{1,0:T(8,128)} %bitcast.8, f32[192,2048]{1,0:T(8,128)} %pool_ref.1, s32[8,128]{1,0:T(8,128)} %bitcast.9, s32[8,128]{1,0:T(8,128)} %bitcast.10), custom_call_target="tpu_custom_call" | custom-call | tf_op jit(solution)/shard_map/retriever_step/pallas_call | solution.py:748
  105.6 2.8 %results.1 = (f32[1,128]{1,0:T(1,128)}, f32[192,128]{1,0:T(8,128)}, f32[192,128]{1,0:T(8,128)}, f32[192,2048]{1,0:T(8,128)}) custom-call(f32[1,128]{1,0:T(1,128)} %get-tuple-element.12.refs_0_, f32[192,128]{1,0:T(8,128)} %get-tuple-element.13.refs_1_, f32[192,128]{1,0:T(8,128)} %get-tuple-element.14.refs_2_, f32[192,2048]{1,0:T(8,128)} %get-tuple-element.15.refs_3_), custom_call_target="tpu_custom_call" | custom-call | tf_op jit(solution)/shard_map/results/pallas_call | solution.py:764

commit v4 on v3

--- a/solution.py
+++ b/solution.py
@@ -79,7 +79,7 @@
 
 
 REQ, ROWS, QUERY, PROB = range(4)
-SIB_D, SIB_Q, SIB_H, SIB_G, SIB_DD, SIB_P, PART_Q, PART_DQ, PART_L = range(9)
+SIB_D, SIB_Q, SIB_H, _, SIB_DD, SIB_P, PART_Q, PART_DQ, PART_L = range(9)
 DOC_1, DOC_2, GRAD_1, GRAD_2 = range(4)
 
 
@@ -89,9 +89,9 @@
     idx_mine, idx_all, q_part, q_all, q_re, d_nat, d_sib, d_raw, d_all, lr_all, sid,
     rq_out, rq_in, lt, pool_s,
     p_out, p_in, p_all, f_out, f_in, hs_mine, hs_sib, hq, st, ch, stat_out, stat_in,
-    hc_out, hc_in, g3_out, c1x, c1y, cx, cy, c2x, c2y, dd_out, dd_sib, dd_nat, g_sib_out, g_sib_in, g_out, g_in, wcat, at_s,
+    hc_out, hc_in, g3_out, c1x, c1y, cx, cy, c2x, c2y, dd_out, dd_sib, dd_nat, g_sib_out, g_sib_in, g_out, g_in, hots_t, hp, at_s,
     dq_out, dq_in, loss_out, loss_in, pos_out, pos_in, lrow,
-    plane_s, plane_r, x_s, x_r, y_s, y_r, row_s, row_r, idx_s, idx_r, qs, qr, gs, gr, one_s, one_r,
+    plane_s, plane_r, x_s, x_r, y_s, y_r, row_s, row_r, idx_s, idx_r, qs, qr, gs, gr, sg_s, sg_r, one_s, one_r,
 ):
     blk, dim = lax.axis_index("blk"), lax.axis_index("dim")
     xy, z = blk // 8, blk % 8
@@ -191,13 +191,6 @@
         doc_y1((y + k + 1) % 4, y).start()
 
     loop(3, doc_first)
-
-    @pl.when(holder)
-    def _():
-        remote(q_ref, q_part, one_s.at[PART_Q], one_r.at[PART_Q], partner).wait_recv()
-        own, other = upright(q_ref[...]), upright(q_part[...])
-        q_all[c, t] = fold(jnp.where(yh == 0, own, other), jnp.where(yh == 0, other, own))
-        loop(7, lambda k: q_copy((z + k + 1) % 8).start())
 
     def idx_wait(tt):
         @pl.when(2 * tt + yh != z)
@@ -247,6 +240,13 @@
 
     loop(15, lambda k: req_copy((me_p + k + 1) % 16, me_p).start())
 
+    @pl.when(holder)
+    def _():
+        remote(q_ref, q_part, one_s.at[PART_Q], one_r.at[PART_Q], partner).wait_recv()
+        own, other = upright(q_ref[...]), upright(q_part[...])
+        q_all[c, t] = fold(jnp.where(yh == 0, own, other), jnp.where(yh == 0, other, own))
+        loop(7, lambda k: q_copy((z + k + 1) % 8).start())
+
     def doc_second(k):
         xx, yy = (x + k + 1) % 4, (y + k + 1) % 4
         doc_x1(xx, xx).wait_recv()
@@ -415,8 +415,12 @@
         p_all[k, 64:128] = last
 
     loop(8, rearrange_d)
-    filler = jnp.zeros((120, 512), F32)
-    sid_t = jnp.concatenate([sid[...], filler], axis=0).T
+    sid_t = jnp.concatenate([sid[...], jnp.zeros((120, 512), F32)], axis=0).T
+    lane512 = lax.broadcasted_iota(jnp.int32, (512, 128), 1).astype(F32)
+    for a in range(8):
+        hots_t[:, a * 128 : (a + 1) * 128] = jnp.where(
+            sid_t[:, a : a + 1] == lane512, 1.0, 0.0
+        ).astype(BF16)
 
     def stat_wait(k):
         r = (me_r + k + 1) % 16
@@ -432,6 +436,23 @@
 
     hq[...] = jnp.exp(hq[...] - log_total)
 
+    shares = columns(hq)
+    chances = shares.T
+    for a in range(8):
+        hc_out[a] = chances[a : a + 1, :]
+    hc_in[me_p] = hc_out[xy]
+
+    def prob_copy(p, slot):
+        return remote(
+            hc_out.at[p // 2], hc_in.at[slot], plane_s.at[PROB, p], plane_r.at[PROB, slot], plane_dev(p)
+        )
+
+    loop(15, lambda k: prob_copy((me_p + k + 1) % 16, me_p).start())
+
+    for a in range(8):
+        for k, part in enumerate(split3(p_all[a] * shares[:, a : a + 1])):
+            hp[k, a] = part
+
     def chance(j):
         rows = pl.ds(pl.multiple_of(j * 128, 128), 128)
         value = jnp.exp(st[rows, :] - log_total)
@@ -440,29 +461,29 @@
 
     loop(4, chance)
 
-    g_sib_out[...] = mm(ch[...], d_all[1 - c].reshape(512, 384), NN, HIGHEST)
-    sib_g = remote(g_sib_out, g_sib_in, one_s.at[SIB_G], one_r.at[SIB_G], sibling)
-    sib_g.start()
-    hc_t = jnp.concatenate([hq[...], filler], axis=0).T
-    lane512 = lax.broadcasted_iota(jnp.int32, (512, 128), 1).astype(F32)
-    for a in range(8):
-        wcat[:, a * 128 : (a + 1) * 128] = jnp.where(
-            sid_t[:, a : a + 1] == lane512, hc_t[:, a : a + 1], 0.0
-        )
-    g_own = mm(ch[...], d_all[c].reshape(512, 384), NN, HIGHEST)
-    g_own = g_own + mm(wcat[...], p_all[...].reshape(1024, 384), NN, HIGHEST)
-    sib_g.wait_recv()
-    g_out[...] = (g_own + g_sib_in[...]).reshape(4, 128, 384)
+    def sib_g(h):
+        return remote(g_sib_out.at[h], g_sib_in.at[h], sg_s.at[h], sg_r.at[h], sibling)
 
     def grad_copy(tt, slot):
         return remote(g_out.at[tt], g_in.at[slot], gs.at[tt], gr.at[slot], z_dev(2 * tt + yh))
 
-    def grad_send(tt):
-        @pl.when(2 * tt + yh != z)
-        def _():
-            grad_copy(tt, z).start()
-
-    loop(4, grad_send)
+    def grad_half(h):
+        rows = pl.ds(pl.multiple_of(h * 256, 256), 256)
+        g_sib_out[h] = mm(ch[rows, :], d_all[1 - c].reshape(512, 384), NN, HIGHEST)
+        sib_g(h).start()
+        g_own = mm(ch[rows, :], d_all[c].reshape(512, 384), NN, HIGHEST)
+        for k in range(3):
+            g_own = g_own + mm(hots_t[rows, :], hp[k].reshape(1024, 384), NN)
+        sib_g(h).wait_recv()
+        g_out[pl.ds(h * 2, 2)] = (g_own + g_sib_in[h]).reshape(2, 128, 384)
+        for i in range(2):
+            tt = h * 2 + i
+
+            @pl.when(2 * tt + yh != z)
+            def _():
+                grad_copy(tt, z).start()
+
+    loop(2, grad_half)
 
     @pl.when(holder)
     def _():
@@ -499,18 +520,6 @@
         grad_x1((x + k + 1) % 4, x).start()
 
     loop(3, grad_first)
-    chances = columns(hq).T
-    for a in range(8):
-        hc_out[a] = chances[a : a + 1, :]
-    hc_in[me_p] = hc_out[xy]
-
-    def prob_copy(p, slot):
-        return remote(
-            hc_out.at[p // 2], hc_in.at[slot], plane_s.at[PROB, p], plane_r.at[PROB, slot], plane_dev(p)
-        )
-
-    loop(15, lambda k: prob_copy((me_p + k + 1) % 16, me_p).start())
-
     def query_wait(k):
         p = (me_p + k + 1) % 16
         query_copy(p, p).wait_recv()
@@ -571,6 +580,63 @@
 
     loop(3, grad_on)
     loop(4, lambda n: pool_grad(n + 4))
+
+    def grad_wait(k):
+        xx, yy = (x + k + 1) % 4, (y + k + 1) % 4
+        grad_x2(xx, xx).wait_recv()
+        grad_y2(yy, yy).wait_recv()
+
+    loop(3, grad_wait)
+    upper_rows = (cy[x] + c2x[(x + 1) % 4]) + (c2x[(x + 2) % 4] + c2x[(x + 3) % 4])
+    lower_rows = (cx[yh, yl] + c2y[(y + 1) % 4]) + (c2y[(y + 2) % 4] + c2y[(y + 3) % 4])
+    value = jnp.concatenate([upper_rows, lower_rows], axis=0)
+    first, last = unfold(value)
+    dd_out[...] = jnp.where(c == 0, last, first)
+    sib_dd = remote(dd_out, dd_sib, one_s.at[SIB_DD], one_r.at[SIB_DD], sibling)
+    sib_dd.start()
+    dd_nat[pl.ds(pl.multiple_of(c * 64, 64), 64), :] = jnp.where(c == 0, first, last)
+
+    sib_d.wait_send()
+    sib_q.wait_send()
+    sib_h.wait_send()
+    loop(2, lambda h: sib_g(h).wait_send())
+
+    def sent(k):
+        p = (me_p + k + 1) % 16
+        for copy in (req_copy, rows_copy, query_copy, prob_copy):
+            copy(p, me_p).wait_send()
+        stat_copy((me_r + k + 1) % 16, me_r).wait_send()
+
+    loop(15, sent)
+
+    def sent4(k):
+        for copy in (doc_x1, doc_x2, grad_x1, grad_x2):
+            copy((x + k + 1) % 4, x).wait_send()
+        for copy in (doc_y1, doc_y2, grad_y1, grad_y2):
+            copy((y + k + 1) % 4, y).wait_send()
+
+    loop(3, sent4)
+    sib_p.wait_send()
+
+    def grad_sent(tt):
+        @pl.when(2 * tt + yh != z)
+        def _():
+            grad_copy(tt, z).wait_send()
+
+    loop(4, grad_sent)
+
+    @pl.when(holder)
+    def _():
+        def z_sent(k):
+            zz = (z + k + 1) % 8
+            idx_copy(zz).wait_send()
+            q_copy(zz).wait_send()
+
+        loop(7, z_sent)
+
+    @pl.when(jnp.logical_not(holder))
+    def _():
+        part_q.wait_send()
 
     part_dq = remote(dq_out, dq_in, one_s.at[PART_DQ], one_r.at[PART_DQ], partner)
     part_l = remote(loss_out, loss_in, one_s.at[PART_L], one_r.at[PART_L], partner)
@@ -595,20 +661,9 @@
         dq_ref[...] = (jnp.where(yh == 0, first, last).T[0:192] - d_ref[...]) * SCALE
         loss_ref[...] = loss_out[...]
 
-    def grad_wait(k):
-        xx, yy = (x + k + 1) % 4, (y + k + 1) % 4
-        grad_x2(xx, xx).wait_recv()
-        grad_y2(yy, yy).wait_recv()
-
-    loop(3, grad_wait)
-    upper_rows = (cy[x] + c2x[(x + 1) % 4]) + (c2x[(x + 2) % 4] + c2x[(x + 3) % 4])
-    lower_rows = (cx[yh, yl] + c2y[(y + 1) % 4]) + (c2y[(y + 2) % 4] + c2y[(y + 3) % 4])
-    value = jnp.concatenate([upper_rows, lower_rows], axis=0)
-    first, last = unfold(value)
-    dd_out[...] = jnp.where(c == 0, last, first)
-    sib_dd = remote(dd_out, dd_sib, one_s.at[SIB_DD], one_r.at[SIB_DD], sibling)
-    sib_dd.start()
-    dd_nat[pl.ds(pl.multiple_of(c * 64, 64), 64), :] = jnp.where(c == 0, first, last)
+    sib_dd.wait_recv()
+    dd_nat[pl.ds(pl.multiple_of((1 - c) * 64, 64), 64), :] = dd_sib[...]
+    dd_ref[...] = (dd_nat[...].T[0:192] - q_ref[...]) * SCALE
 
     @pl.when(jnp.logical_not(holder))
     def _():
@@ -617,54 +672,12 @@
         part_dq.wait_recv()
         dq_ref[...] = (dq_in[...] - d_ref[...]) * SCALE
 
-    sib_dd.wait_recv()
-    dd_nat[pl.ds(pl.multiple_of((1 - c) * 64, 64), 64), :] = dd_sib[...]
-    dd_ref[...] = (dd_nat[...].T[0:192] - q_ref[...]) * SCALE
-
-    sib_d.wait_send()
-    sib_q.wait_send()
-    sib_h.wait_send()
-    sib_g.wait_send()
     sib_dd.wait_send()
 
-    def sent(k):
-        p = (me_p + k + 1) % 16
-        for copy in (req_copy, rows_copy, query_copy, prob_copy):
-            copy(p, me_p).wait_send()
-        stat_copy((me_r + k + 1) % 16, me_r).wait_send()
-
-    loop(15, sent)
-
-    def sent4(k):
-        for copy in (doc_x1, doc_x2, grad_x1, grad_x2):
-            copy((x + k + 1) % 4, x).wait_send()
-        for copy in (doc_y1, doc_y2, grad_y1, grad_y2):
-            copy((y + k + 1) % 4, y).wait_send()
-
-    loop(3, sent4)
-    sib_p.wait_send()
-
-    def grad_sent(tt):
-        @pl.when(2 * tt + yh != z)
-        def _():
-            grad_copy(tt, z).wait_send()
-
-    loop(4, grad_sent)
-
     @pl.when(holder)
     def _():
-        def z_sent(k):
-            zz = (z + k + 1) % 8
-            idx_copy(zz).wait_send()
-            q_copy(zz).wait_send()
-
-        loop(7, z_sent)
         part_l.wait_send()
         part_dq.wait_send()
-
-    @pl.when(jnp.logical_not(holder))
-    def _():
-        part_q.wait_send()
 
 
 def hand_on(*refs):
@@ -715,11 +728,12 @@
         f(64, 256),
         f(64, 256),
         f(128, 256),
-        f(512, 384),
-        f(512, 384),
+        f(2, 256, 384),
+        f(2, 256, 384),
         f(4, 128, 384),
         f(8, 128, 384),
-        f(512, 1024),
+        pltpu.VMEM((512, 1024), BF16),
+        pltpu.VMEM((3, 8, 128, 384), BF16),
         pltpu.VMEM((2, 192, 2048), BF16),
         f(192, 128),
         f(192, 128),
@@ -742,6 +756,8 @@
         pltpu.SemaphoreType.DMA((4,)),
         pltpu.SemaphoreType.DMA((4,)),
         pltpu.SemaphoreType.DMA((8,)),
+        pltpu.SemaphoreType.DMA((2,)),
+        pltpu.SemaphoreType.DMA((2,)),
         pltpu.SemaphoreType.DMA((9,)),
         pltpu.SemaphoreType.DMA((9,)),
     ]

time: 109 us -> 105 us (0.963)
  the two profiles are of different devices: /device:TPU:1 before, /device:TPU:16 now
where the time goes in v4:
time: 105 us
  Pallas kernels  104 us (99%)
    pallas_call x1, Pallas kernels, per_device(): pl.pallas_call(kernel, name='retriever_step', out_shape=(jax.ShapeDtypeSt...  101 us
    pallas_call x1, Pallas kernels, per_device(): pl.pallas_call(hand_on, name='results', out_shape=tuple((jax.ShapeDtypeSt...  2.79 us

profile of v4, /device:TPU:16, one launch (start us, length us, event | category | flops | bytes accessed | tf_op | source)
XLA Modules:
  0.0 104.6 jit_solution(8333917903165802219)
XLA Ops:
  0.6 101.2 %retriever_step.1 = (f32[1,128]{1,0:T(1,128)}, f32[192,128]{1,0:T(8,128)}, f32[192,128]{1,0:T(8,128)}, f32[192,2048]{1,0:T(8,128)}) custom-call(f32[192,128]{1,0:T(8,128)} %bitcast.7, f32[192,128]{1,0:T(8,128)} %bitcast.8, f32[192,2048]{1,0:T(8,128)} %pool_ref.1, s32[8,128]{1,0:T(8,128)} %bitcast.9, s32[8,128]{1,0:T(8,128)} %bitcast.10), custom_call_target="tpu_custom_call" | custom-call | tf_op jit(solution)/shard_map/retriever_step/pallas_call | solution.py:764
  101.8 2.8 %results.1 = (f32[1,128]{1,0:T(1,128)}, f32[192,128]{1,0:T(8,128)}, f32[192,128]{1,0:T(8,128)}, f32[192,2048]{1,0:T(8,128)}) custom-call(f32[1,128]{1,0:T(1,128)} %get-tuple-element.12.refs_0_, f32[192,128]{1,0:T(8,128)} %get-tuple-element.13.refs_1_, f32[192,128]{1,0:T(8,128)} %get-tuple-element.14.refs_2_, f32[192,2048]{1,0:T(8,128)} %get-tuple-element.15.refs_3_), custom_call_target="tpu_custom_call" | custom-call | tf_op jit(solution)/shard_map/results/pallas_call | solution.py:780

commit v5 on v4

--- a/solution.py
+++ b/solution.py
@@ -79,7 +79,7 @@
 
 
 REQ, ROWS, QUERY, PROB = range(4)
-SIB_D, SIB_Q, SIB_H, _, SIB_DD, SIB_P, PART_Q, PART_DQ, PART_L = range(9)
+SIB_D, SIB_Q, SIB_H, SIB_G, SIB_DD, SIB_P, PART_Q, PART_DQ, PART_L = range(9)
 DOC_1, DOC_2, GRAD_1, GRAD_2 = range(4)
 
 
@@ -89,9 +89,9 @@
     idx_mine, idx_all, q_part, q_all, q_re, d_nat, d_sib, d_raw, d_all, lr_all, sid,
     rq_out, rq_in, lt, pool_s,
     p_out, p_in, p_all, f_out, f_in, hs_mine, hs_sib, hq, st, ch, stat_out, stat_in,
-    hc_out, hc_in, g3_out, c1x, c1y, cx, cy, c2x, c2y, dd_out, dd_sib, dd_nat, g_sib_out, g_sib_in, g_out, g_in, hots_t, hp, at_s,
+    hc_out, hc_in, g3_out, c1x, c1y, cx, cy, c2x, c2y, dd_out, dd_sib, dd_nat, g_sib_out, g_sib_in, g_own, g_hard, scales, g_out, g_in, hots_t, hp, at_s,
     dq_out, dq_in, loss_out, loss_in, pos_out, pos_in, lrow,
-    plane_s, plane_r, x_s, x_r, y_s, y_r, row_s, row_r, idx_s, idx_r, qs, qr, gs, gr, sg_s, sg_r, one_s, one_r,
+    plane_s, plane_r, x_s, x_r, y_s, y_r, row_s, row_r, idx_s, idx_r, qs, qr, gs, gr, one_s, one_r,
 ):
     blk, dim = lax.axis_index("blk"), lax.axis_index("dim")
     xy, z = blk // 8, blk % 8
@@ -240,25 +240,25 @@
 
     loop(15, lambda k: req_copy((me_p + k + 1) % 16, me_p).start())
 
+    def doc_second(k):
+        xx, yy = (x + k + 1) % 4, (y + k + 1) % 4
+        doc_x1(xx, xx).wait_recv()
+        doc_y1(yy, yy).wait_recv()
+
+    loop(3, doc_second)
+
+    def doc_on(k):
+        doc_y2((y + k + 1) % 4, y).start()
+        doc_x2((x + k + 1) % 4, x).start()
+
+    loop(3, doc_on)
+
     @pl.when(holder)
     def _():
         remote(q_ref, q_part, one_s.at[PART_Q], one_r.at[PART_Q], partner).wait_recv()
         own, other = upright(q_ref[...]), upright(q_part[...])
         q_all[c, t] = fold(jnp.where(yh == 0, own, other), jnp.where(yh == 0, other, own))
         loop(7, lambda k: q_copy((z + k + 1) % 8).start())
-
-    def doc_second(k):
-        xx, yy = (x + k + 1) % 4, (y + k + 1) % 4
-        doc_x1(xx, xx).wait_recv()
-        doc_y1(yy, yy).wait_recv()
-
-    loop(3, doc_second)
-
-    def doc_on(k):
-        doc_y2((y + k + 1) % 4, y).start()
-        doc_x2((x + k + 1) % 4, x).start()
-
-    loop(3, doc_on)
 
     def req_wait(k):
         p = (me_p + k + 1) % 16
@@ -350,6 +350,33 @@
     best = lax.fori_loop(0, 8, top, jnp.full((8, 512), -jnp.inf, F32))
     best = jnp.max(best, axis=0, keepdims=True)
 
+    square = st[pl.ds(pl.multiple_of(xy * 64, 64), 64), pl.ds(pl.multiple_of(t * 128, 128), 128)]
+    on_diagonal = lax.broadcasted_iota(jnp.int32, (64, 128), 1) == (
+        lax.broadcasted_iota(jnp.int32, (64, 128), 0) + c * 64
+    )
+    positive = jnp.sum(jnp.where(on_diagonal, square, 0.0), axis=0, keepdims=True)
+    pos_out[:, 0:128] = positive
+    pos_out[:, 128:640] = best
+    sib_p = remote(pos_out, pos_in, one_s.at[SIB_P], one_r.at[SIB_P], sibling)
+
+    def weigh(j, total):
+        rows = pl.ds(pl.multiple_of(j * 128, 128), 128)
+        value = jnp.exp(st[rows, :] - best)
+        st[rows, :] = value
+        ch[:, rows] = value.T
+        return total + jnp.sum(value.reshape(16, 8, 512), axis=0)
+
+    weight = lax.fori_loop(0, 4, weigh, jnp.zeros((8, 512), F32))
+    weight = jnp.sum(weight, axis=0, keepdims=True)
+
+    def rearrange_d(k):
+        first, last = regroup(d_raw[0, k // 2, k % 2], d_raw[1, k // 2, k % 2])
+        d_all[0, k] = first
+        d_all[1, k] = last
+
+    loop(8, rearrange_d)
+    sib_p.start()
+
     def rows_wait(k):
         p = (me_p + k + 1) % 16
         rows_copy(p, p).wait_recv()
@@ -375,27 +402,20 @@
 
     loop(15, lambda k: query_copy((me_p + k + 1) % 16, me_p).start())
 
+    g_sib_out[...] = mm(ch[...], d_all[1 - c].reshape(512, 384), NN, HIGHEST)
+    sib_g = remote(g_sib_out, g_sib_in, one_s.at[SIB_G], one_r.at[SIB_G], sibling)
+    sib_g.start()
+
     sib_h.wait_recv()
     hard = (hs_mine[...] + hs_sib[...]) * SCALE
     for a in range(8):
         row = jnp.sum(jnp.where(hot(a), hard[:, a : a + 1], 0.0), axis=0, keepdims=True)
         hq[a : a + 1, :] = jnp.where(sid[a : a + 1, :] >= 0.0, row, -jnp.inf)
     peak = jnp.maximum(best, jnp.max(hq[...], axis=0, keepdims=True))
-
-    def add(j, total):
-        rows = jnp.exp(st[pl.ds(pl.multiple_of(j * 64, 64), 64), :] - peak)
-        return total + jnp.sum(rows.reshape(8, 8, 512), axis=0)
-
-    total = lax.fori_loop(0, 8, add, jnp.zeros((8, 512), F32))
-    total = total + jnp.exp(hq[...] - peak) * jnp.where(c == 0, 1.0, 0.0)
-    total = jnp.sum(total, axis=0, keepdims=True)
-    square = st[pl.ds(pl.multiple_of(xy * 64, 64), 64), pl.ds(pl.multiple_of(t * 128, 128), 128)]
-    on_diagonal = lax.broadcasted_iota(jnp.int32, (64, 128), 1) == (
-        lax.broadcasted_iota(jnp.int32, (64, 128), 0) + c * 64
-    )
-    positive = jnp.sum(jnp.where(on_diagonal, square, 0.0), axis=0, keepdims=True)
-    pos_out[...] = positive
-    sib_p = remote(pos_out, pos_in, one_s.at[SIB_P], one_r.at[SIB_P], sibling)
+    hq[...] = jnp.exp(hq[...] - peak)
+    total = jnp.sum(hq[...], axis=0, keepdims=True) * jnp.where(c == 0, 1.0, 0.0)
+    total = total + weight * jnp.exp(best - peak)
+
     stat_out[:, 0:512] = peak
     stat_out[:, 512:1024] = total
     stat_in[me_r] = stat_out[...]
@@ -404,17 +424,13 @@
         return remote(stat_out, stat_in.at[slot], row_s.at[r], row_r.at[slot], row_dev(r))
 
     loop(15, lambda k: stat_copy((me_r + k + 1) % 16, me_r).start())
-    sib_p.start()
-
-    def rearrange_d(k):
-        first, last = regroup(d_raw[0, k // 2, k % 2], d_raw[1, k // 2, k % 2])
-        d_all[0, k] = first
-        d_all[1, k] = last
+
+    def rearrange_p(k):
         first, last = regroup(p_in[0, k], p_in[1, k])
         p_all[k, 0:64] = first
         p_all[k, 64:128] = last
 
-    loop(8, rearrange_d)
+    loop(8, rearrange_p)
     sid_t = jnp.concatenate([sid[...], jnp.zeros((120, 512), F32)], axis=0).T
     lane512 = lax.broadcasted_iota(jnp.int32, (512, 128), 1).astype(F32)
     for a in range(8):
@@ -422,6 +438,17 @@
             sid_t[:, a : a + 1] == lane512, 1.0, 0.0
         ).astype(BF16)
 
+    shares = columns(hq)
+    for a in range(8):
+        for k, part in enumerate(split3(p_all[a] * shares[:, a : a + 1])):
+            hp[k, a] = part
+    g_hard[...] = (
+        mm(hots_t[...], hp[0].reshape(1024, 384), NN)
+        + mm(hots_t[...], hp[1].reshape(1024, 384), NN)
+        + mm(hots_t[...], hp[2].reshape(1024, 384), NN)
+    )
+    g_own[...] = mm(ch[...], d_all[c].reshape(512, 384), NN, HIGHEST)
+
     def stat_wait(k):
         r = (me_r + k + 1) % 16
         stat_copy(r, r).wait_recv()
@@ -429,15 +456,40 @@
     loop(15, stat_wait)
     peaks = jnp.concatenate([stat_in[r, :, 0:512] for r in range(16)], axis=0)
     totals = jnp.concatenate([stat_in[r, :, 512:1024] for r in range(16)], axis=0)
-    peak = jnp.max(peaks, axis=0, keepdims=True)
-    total = jnp.sum(totals * jnp.exp(peaks - peak), axis=0, keepdims=True)
-    log_total = peak + jnp.log(total)
+    most = jnp.max(peaks, axis=0, keepdims=True)
+    total = jnp.sum(totals * jnp.exp(peaks - most), axis=0, keepdims=True)
+    log_total = most + jnp.log(total)
     lrow[...] = log_total
 
-    hq[...] = jnp.exp(hq[...] - log_total)
-
-    shares = columns(hq)
-    chances = shares.T
+    sib_p.wait_recv()
+    to_own = jnp.exp(best - log_total)
+    to_hard = jnp.exp(peak - log_total)
+    to_sib = jnp.exp(pos_in[:, 128:640] - log_total)
+    scales[...] = jnp.concatenate([to_own, to_hard, to_sib, jnp.zeros((125, 512), F32)], axis=0).T
+    sib_g.wait_recv()
+
+    def grad_copy(tt, slot):
+        return remote(g_out.at[tt], g_in.at[slot], gs.at[tt], gr.at[slot], z_dev(2 * tt + yh))
+
+    def grad_send(tt):
+        rows = pl.ds(pl.multiple_of(tt * 128, 128), 128)
+        by = scales[rows, :]
+        g_out[tt] = (
+            g_own[rows, :] * by[:, 0:1] + g_sib_in[rows, :] * by[:, 2:3]
+        ) + g_hard[rows, :] * by[:, 1:2]
+
+        @pl.when(2 * tt + yh != z)
+        def _():
+            grad_copy(tt, z).start()
+
+    loop(4, grad_send)
+
+    @pl.when(holder)
+    def _():
+        g_in[z] = g_out[t]
+
+    hq[...] = hq[...] * to_hard
+    chances = columns(hq).T
     for a in range(8):
         hc_out[a] = chances[a : a + 1, :]
     hc_in[me_p] = hc_out[xy]
@@ -449,45 +501,11 @@
 
     loop(15, lambda k: prob_copy((me_p + k + 1) % 16, me_p).start())
 
-    for a in range(8):
-        for k, part in enumerate(split3(p_all[a] * shares[:, a : a + 1])):
-            hp[k, a] = part
-
     def chance(j):
         rows = pl.ds(pl.multiple_of(j * 128, 128), 128)
-        value = jnp.exp(st[rows, :] - log_total)
-        st[rows, :] = value
-        ch[:, rows] = value.T
+        st[rows, :] = st[rows, :] * to_own
 
     loop(4, chance)
-
-    def sib_g(h):
-        return remote(g_sib_out.at[h], g_sib_in.at[h], sg_s.at[h], sg_r.at[h], sibling)
-
-    def grad_copy(tt, slot):
-        return remote(g_out.at[tt], g_in.at[slot], gs.at[tt], gr.at[slot], z_dev(2 * tt + yh))
-
-    def grad_half(h):
-        rows = pl.ds(pl.multiple_of(h * 256, 256), 256)
-        g_sib_out[h] = mm(ch[rows, :], d_all[1 - c].reshape(512, 384), NN, HIGHEST)
-        sib_g(h).start()
-        g_own = mm(ch[rows, :], d_all[c].reshape(512, 384), NN, HIGHEST)
-        for k in range(3):
-            g_own = g_own + mm(hots_t[rows, :], hp[k].reshape(1024, 384), NN)
-        sib_g(h).wait_recv()
-        g_out[pl.ds(h * 2, 2)] = (g_own + g_sib_in[h]).reshape(2, 128, 384)
-        for i in range(2):
-            tt = h * 2 + i
-
-            @pl.when(2 * tt + yh != z)
-            def _():
-                grad_copy(tt, z).start()
-
-    loop(2, grad_half)
-
-    @pl.when(holder)
-    def _():
-        g_in[z] = g_out[t]
 
     def doc_grad(part):
         value = mm(st[...], q_re[part].reshape(512, 384), NN, HIGHEST)
@@ -520,6 +538,7 @@
         grad_x1((x + k + 1) % 4, x).start()
 
     loop(3, grad_first)
+
     def query_wait(k):
         p = (me_p + k + 1) % 16
         query_copy(p, p).wait_recv()
@@ -599,7 +618,7 @@
     sib_d.wait_send()
     sib_q.wait_send()
     sib_h.wait_send()
-    loop(2, lambda h: sib_g(h).wait_send())
+    sib_g.wait_send()
 
     def sent(k):
         p = (me_p + k + 1) % 16
@@ -640,11 +659,12 @@
 
     part_dq = remote(dq_out, dq_in, one_s.at[PART_DQ], one_r.at[PART_DQ], partner)
     part_l = remote(loss_out, loss_in, one_s.at[PART_L], one_r.at[PART_L], partner)
-    sib_p.wait_recv()
 
     @pl.when(holder)
     def _():
-        loss_out[...] = lrow[:, pl.ds(pl.multiple_of(t * 128, 128), 128)] - (pos_out[...] + pos_in[...])
+        loss_out[...] = lrow[:, pl.ds(pl.multiple_of(t * 128, 128), 128)] - (
+            pos_out[:, 0:128] + pos_in[:, 0:128]
+        )
         part_l.start()
 
         def wait(k):
@@ -728,8 +748,11 @@
         f(64, 256),
         f(64, 256),
         f(128, 256),
-        f(2, 256, 384),
-        f(2, 256, 384),
+        f(512, 384),
+        f(512, 384),
+        f(512, 384),
+        f(512, 384),
+        f(512, 128),
         f(4, 128, 384),
         f(8, 128, 384),
         pltpu.VMEM((512, 1024), BF16),
@@ -739,8 +762,8 @@
         f(192, 128),
         f(1, 128),
         f(1, 128),
-        f(1, 128),
-        f(1, 128),
+        f(1, 640),
+        f(1, 640),
         f(1, 512),
         pltpu.SemaphoreType.DMA((4, 16)),
         pltpu.SemaphoreType.DMA((4, 16)),
@@ -756,8 +779,6 @@
         pltpu.SemaphoreType.DMA((4,)),
         pltpu.SemaphoreType.DMA((4,)),
         pltpu.SemaphoreType.DMA((8,)),
-        pltpu.SemaphoreType.DMA((2,)),
-        pltpu.SemaphoreType.DMA((2,)),
         pltpu.SemaphoreType.DMA((9,)),
         pltpu.SemaphoreType.DMA((9,)),
     ]

time: 105 us -> 109 us (1.038)
  the two profiles are of different devices: /device:TPU:16 before, /device:TPU:80 now
where the time goes in v5:
time: 109 us
  Pallas kernels  108 us (99%)
    pallas_call x1, Pallas kernels, per_device(): pl.pallas_call(kernel, name='retriever_step', out_shape=(jax.ShapeDtypeSt...  106 us
    pallas_call x1, Pallas kernels, per_device(): pl.pallas_call(hand_on, name='results', out_shape=tuple((jax.ShapeDtypeSt...  2.79 us

profile of v5, /device:TPU:80, one launch (start us, length us, event | category | flops | bytes accessed | tf_op | source)
XLA Modules:
  0.0 109.0 jit_solution(1564709208118958375)
XLA Ops:
  0.6 105.6 %retriever_step.1 = (f32[1,128]{1,0:T(1,128)}, f32[192,128]{1,0:T(8,128)}, f32[192,128]{1,0:T(8,128)}, f32[192,2048]{1,0:T(8,128)}) custom-call(f32[192,128]{1,0:T(8,128)} %bitcast.7, f32[192,128]{1,0:T(8,128)} %bitcast.8, f32[192,2048]{1,0:T(8,128)} %pool_ref.1, s32[8,128]{1,0:T(8,128)} %bitcast.9, s32[8,128]{1,0:T(8,128)} %bitcast.10), custom_call_target="tpu_custom_call" | custom-call | tf_op jit(solution)/shard_map/retriever_step/pallas_call | solution.py:785
  106.2 2.8 %results.1 = (f32[1,128]{1,0:T(1,128)}, f32[192,128]{1,0:T(8,128)}, f32[192,128]{1,0:T(8,128)}, f32[192,2048]{1,0:T(8,128)}) custom-call(f32[1,128]{1,0:T(1,128)} %get-tuple-element.12.refs_0_, f32[192,128]{1,0:T(8,128)} %get-tuple-element.13.refs_1_, f32[192,128]{1,0:T(8,128)} %get-tuple-element.14.refs_2_, f32[192,2048]{1,0:T(8,128)} %get-tuple-element.15.refs_3_), custom_call_target="tpu_custom_call" | custom-call | tf_op jit(solution)/shard_map/results/pallas_call | solution.py:801

commit v6 on v4

--- a/solution.py
+++ b/solution.py
@@ -89,7 +89,7 @@
     idx_mine, idx_all, q_part, q_all, q_re, d_nat, d_sib, d_raw, d_all, lr_all, sid,
     rq_out, rq_in, lt, pool_s,
     p_out, p_in, p_all, f_out, f_in, hs_mine, hs_sib, hq, st, ch, stat_out, stat_in,
-    hc_out, hc_in, g3_out, c1x, c1y, cx, cy, c2x, c2y, dd_out, dd_sib, dd_nat, g_sib_out, g_sib_in, g_out, g_in, hots_t, hp, at_s,
+    hc_out, hc_in, g3_out, c1x, c1y, cx, cy, c2x, c2y, dd_out, dd_sib, dd_nat, g_sib_out, g_sib_in, g_out, g_in, hots_t, hp, at_s, hots_r,
     dq_out, dq_in, loss_out, loss_in, pos_out, pos_in, lrow,
     plane_s, plane_r, x_s, x_r, y_s, y_r, row_s, row_r, idx_s, idx_r, qs, qr, gs, gr, sg_s, sg_r, one_s, one_r,
 ):
@@ -281,6 +281,7 @@
             col = jnp.sum(jnp.where(lane128 == g * 4 + i, lt[...], 0.0), axis=1, keepdims=True)
             hots.append(jnp.where(col == lane2048, 1.0, 0.0).astype(BF16))
         hots = jnp.concatenate(hots, axis=0)
+        hots_r[pl.ds(pl.multiple_of(g * 512, 512), 512), :] = hots
         got = mm(hots, pool_s[0], NT) + mm(hots, pool_s[1], NT) + mm(hots, pool_s[2], NT)
         for i in range(4):
             p = g * 4 + i
@@ -533,22 +534,14 @@
         rows = jnp.concatenate(unfold(f_in[i]), axis=0) * (col * SCALE)
         terms = split3(rows.T[0:192])
         for k in range(2):
-            at_s[k, :, pl.ds(pl.multiple_of(i * 128, 128), 128)] = terms[k]
+            at_s[k * 192 : k * 192 + 192, pl.ds(pl.multiple_of(i * 128, 128), 128)] = terms[k]
 
     loop(16, turn)
-    lane256 = lax.broadcasted_iota(jnp.int32, (128, 256), 1).astype(F32) + 1.0
 
     def pool_grad(n):
-        base = (n * 256).astype(F32)
-        hots = jnp.concatenate(
-            [
-                jnp.where(lt[:, i : i + 1] == lane256 + base, 1.0, 0.0).astype(BF16)
-                for i in range(16)
-            ],
-            axis=0,
-        )
-        value = mm(at_s[0], hots, NN) + mm(at_s[1], hots, NN)
-        gp_ref[:, pl.ds(pl.multiple_of(n * 256, 256), 256)] = value
+        columns_n = pl.ds(pl.multiple_of(n * 256, 256), 256)
+        value = mm(at_s[...], hots_r[:, columns_n], NN)
+        gp_ref[:, columns_n] = value[0:192] + value[192:384]
 
     loop(4, pool_grad)
 
@@ -734,7 +727,8 @@
         f(8, 128, 384),
         pltpu.VMEM((512, 1024), BF16),
         pltpu.VMEM((3, 8, 128, 384), BF16),
-        pltpu.VMEM((2, 192, 2048), BF16),
+        pltpu.VMEM((384, 2048), BF16),
+        pltpu.VMEM((2048, 2048), BF16),
         f(192, 128),
         f(192, 128),
         f(1, 128),

time: 105 us -> 105 us (level)
  no operation moved by 1% of the time
where the time goes in v6:
time: 105 us; the launch traced here: 104 us
  Pallas kernels  103 us (98%)
    pallas_call x1, Pallas kernels, per_device(): pl.pallas_call(kernel, name='retriever_step', out_shape=(jax.ShapeDtypeSt...  100 us
    pallas_call x1, Pallas kernels, per_device(): pl.pallas_call(hand_on, name='results', out_shape=tuple((jax.ShapeDtypeSt...  2.79 us

profile of v6, /device:TPU:16, one launch (start us, length us, event | category | flops | bytes accessed | tf_op | source)
XLA Modules:
  0.0 103.6 jit_solution(6447663539270458777)
XLA Ops:
  0.6 100.2 %retriever_step.1 = (f32[1,128]{1,0:T(1,128)}, f32[192,128]{1,0:T(8,128)}, f32[192,128]{1,0:T(8,128)}, f32[192,2048]{1,0:T(8,128)}) custom-call(f32[192,128]{1,0:T(8,128)} %bitcast.7, f32[192,128]{1,0:T(8,128)} %bitcast.8, f32[192,2048]{1,0:T(8,128)} %pool_ref.1, s32[8,128]{1,0:T(8,128)} %bitcast.9, s32[8,128]{1,0:T(8,128)} %bitcast.10), custom_call_target="tpu_custom_call" | custom-call | tf_op jit(solution)/shard_map/retriever_step/pallas_call | solution.py:758
  100.8 2.8 %results.1 = (f32[1,128]{1,0:T(1,128)}, f32[192,128]{1,0:T(8,128)}, f32[192,128]{1,0:T(8,128)}, f32[192,2048]{1,0:T(8,128)}) custom-call(f32[1,128]{1,0:T(1,128)} %get-tuple-element.12.refs_0_, f32[192,128]{1,0:T(8,128)} %get-tuple-element.13.refs_1_, f32[192,128]{1,0:T(8,128)} %get-tuple-element.14.refs_2_, f32[192,2048]{1,0:T(8,128)} %get-tuple-element.15.refs_3_), custom_call_target="tpu_custom_call" | custom-call | tf_op jit(solution)/shard_map/results/pallas_call | solution.py:774

commit v7 on v6

--- a/solution.py
+++ b/solution.py
@@ -438,18 +438,6 @@
     hq[...] = jnp.exp(hq[...] - log_total)
 
     shares = columns(hq)
-    chances = shares.T
-    for a in range(8):
-        hc_out[a] = chances[a : a + 1, :]
-    hc_in[me_p] = hc_out[xy]
-
-    def prob_copy(p, slot):
-        return remote(
-            hc_out.at[p // 2], hc_in.at[slot], plane_s.at[PROB, p], plane_r.at[PROB, slot], plane_dev(p)
-        )
-
-    loop(15, lambda k: prob_copy((me_p + k + 1) % 16, me_p).start())
-
     for a in range(8):
         for k, part in enumerate(split3(p_all[a] * shares[:, a : a + 1])):
             hp[k, a] = part
@@ -489,6 +477,18 @@
     @pl.when(holder)
     def _():
         g_in[z] = g_out[t]
+
+    chances = shares.T
+    for a in range(8):
+        hc_out[a] = chances[a : a + 1, :]
+    hc_in[me_p] = hc_out[xy]
+
+    def prob_copy(p, slot):
+        return remote(
+            hc_out.at[p // 2], hc_in.at[slot], plane_s.at[PROB, p], plane_r.at[PROB, slot], plane_dev(p)
+        )
+
+    loop(15, lambda k: prob_copy((me_p + k + 1) % 16, me_p).start())
 
     def doc_grad(part):
         value = mm(st[...], q_re[part].reshape(512, 384), NN, HIGHEST)

time: 105 us -> 105 us (level)
  no operation moved by 1% of the time
where the time goes in v7:
time: 105 us; the launch traced here: 104 us
  Pallas kernels  103 us (98%)
    pallas_call x1, Pallas kernels, per_device(): pl.pallas_call(kernel, name='retriever_step', out_shape=(jax.ShapeDtypeSt...  100 us
    pallas_call x1, Pallas kernels, per_device(): pl.pallas_call(hand_on, name='results', out_shape=tuple((jax.ShapeDtypeSt...  2.79 us

profile of v7, /device:TPU:16, one launch (start us, length us, event | category | flops | bytes accessed | tf_op | source)
XLA Modules:
  0.0 103.7 jit_solution(7371206894051118514)
XLA Ops:
  0.6 100.2 %retriever_step.1 = (f32[1,128]{1,0:T(1,128)}, f32[192,128]{1,0:T(8,128)}, f32[192,128]{1,0:T(8,128)}, f32[192,2048]{1,0:T(8,128)}) custom-call(f32[192,128]{1,0:T(8,128)} %bitcast.7, f32[192,128]{1,0:T(8,128)} %bitcast.8, f32[192,2048]{1,0:T(8,128)} %pool_ref.1, s32[8,128]{1,0:T(8,128)} %bitcast.9, s32[8,128]{1,0:T(8,128)} %bitcast.10), custom_call_target="tpu_custom_call" | custom-call | tf_op jit(solution)/shard_map/retriever_step/pallas_call | solution.py:758
  100.9 2.8 %results.1 = (f32[1,128]{1,0:T(1,128)}, f32[192,128]{1,0:T(8,128)}, f32[192,128]{1,0:T(8,128)}, f32[192,2048]{1,0:T(8,128)}) custom-call(f32[1,128]{1,0:T(1,128)} %get-tuple-element.12.refs_0_, f32[192,128]{1,0:T(8,128)} %get-tuple-element.13.refs_1_, f32[192,128]{1,0:T(8,128)} %get-tuple-element.14.refs_2_, f32[192,2048]{1,0:T(8,128)} %get-tuple-element.15.refs_3_), custom_call_target="tpu_custom_call" | custom-call | tf_op jit(solution)/shard_map/results/pallas_call | solution.py:774

commit v8 on v6

--- a/solution.py
+++ b/solution.py
@@ -376,20 +376,6 @@
 
     loop(15, lambda k: query_copy((me_p + k + 1) % 16, me_p).start())
 
-    sib_h.wait_recv()
-    hard = (hs_mine[...] + hs_sib[...]) * SCALE
-    for a in range(8):
-        row = jnp.sum(jnp.where(hot(a), hard[:, a : a + 1], 0.0), axis=0, keepdims=True)
-        hq[a : a + 1, :] = jnp.where(sid[a : a + 1, :] >= 0.0, row, -jnp.inf)
-    peak = jnp.maximum(best, jnp.max(hq[...], axis=0, keepdims=True))
-
-    def add(j, total):
-        rows = jnp.exp(st[pl.ds(pl.multiple_of(j * 64, 64), 64), :] - peak)
-        return total + jnp.sum(rows.reshape(8, 8, 512), axis=0)
-
-    total = lax.fori_loop(0, 8, add, jnp.zeros((8, 512), F32))
-    total = total + jnp.exp(hq[...] - peak) * jnp.where(c == 0, 1.0, 0.0)
-    total = jnp.sum(total, axis=0, keepdims=True)
     square = st[pl.ds(pl.multiple_of(xy * 64, 64), 64), pl.ds(pl.multiple_of(t * 128, 128), 128)]
     on_diagonal = lax.broadcasted_iota(jnp.int32, (64, 128), 1) == (
         lax.broadcasted_iota(jnp.int32, (64, 128), 0) + c * 64
@@ -397,6 +383,25 @@
     positive = jnp.sum(jnp.where(on_diagonal, square, 0.0), axis=0, keepdims=True)
     pos_out[...] = positive
     sib_p = remote(pos_out, pos_in, one_s.at[SIB_P], one_r.at[SIB_P], sibling)
+
+    def weigh(j, total):
+        rows = pl.ds(pl.multiple_of(j * 64, 64), 64)
+        value = jnp.exp(st[rows, :] - best)
+        st[rows, :] = value
+        return total + jnp.sum(value.reshape(8, 8, 512), axis=0)
+
+    weight = lax.fori_loop(0, 8, weigh, jnp.zeros((8, 512), F32))
+    weight = jnp.sum(weight, axis=0, keepdims=True)
+
+    sib_h.wait_recv()
+    hard = (hs_mine[...] + hs_sib[...]) * SCALE
+    for a in range(8):
+        row = jnp.sum(jnp.where(hot(a), hard[:, a : a + 1], 0.0), axis=0, keepdims=True)
+        hq[a : a + 1, :] = jnp.where(sid[a : a + 1, :] >= 0.0, row, -jnp.inf)
+    peak = jnp.maximum(best, jnp.max(hq[...], axis=0, keepdims=True))
+
+    total = jnp.exp(hq[...] - peak) * jnp.where(c == 0, 1.0, 0.0)
+    total = jnp.sum(total, axis=0, keepdims=True) + weight * jnp.exp(best - peak)
     stat_out[:, 0:512] = peak
     stat_out[:, 512:1024] = total
     stat_in[me_r] = stat_out[...]
@@ -454,9 +459,11 @@
         for k, part in enumerate(split3(p_all[a] * shares[:, a : a + 1])):
             hp[k, a] = part
 
+    to_own = jnp.exp(best - log_total)
+
     def chance(j):
         rows = pl.ds(pl.multiple_of(j * 128, 128), 128)
-        value = jnp.exp(st[rows, :] - log_total)
+        value = st[rows, :] * to_own
         st[rows, :] = value
         ch[:, rows] = value.T
 

time: 105 us -> 105 us (level)
  no operation moved by 1% of the time
where the time goes in v8:
time: 105 us; the launch traced here: 104 us
  Pallas kernels  103 us (98%)
    pallas_call x1, Pallas kernels, per_device(): pl.pallas_call(kernel, name='retriever_step', out_shape=(jax.ShapeDtypeSt...  100 us
    pallas_call x1, Pallas kernels, per_device(): pl.pallas_call(hand_on, name='results', out_shape=tuple((jax.ShapeDtypeSt...  2.79 us

profile of v8, /device:TPU:16, one launch (start us, length us, event | category | flops | bytes accessed | tf_op | source)
XLA Modules:
  0.0 103.6 jit_solution(3010298038624084746)
XLA Ops:
  0.6 100.2 %retriever_step.1 = (f32[1,128]{1,0:T(1,128)}, f32[192,128]{1,0:T(8,128)}, f32[192,128]{1,0:T(8,128)}, f32[192,2048]{1,0:T(8,128)}) custom-call(f32[192,128]{1,0:T(8,128)} %bitcast.7, f32[192,128]{1,0:T(8,128)} %bitcast.8, f32[192,2048]{1,0:T(8,128)} %pool_ref.1, s32[8,128]{1,0:T(8,128)} %bitcast.9, s32[8,128]{1,0:T(8,128)} %bitcast.10), custom_call_target="tpu_custom_call" | custom-call | tf_op jit(solution)/shard_map/retriever_step/pallas_call | solution.py:765
  100.8 2.8 %results.1 = (f32[1,128]{1,0:T(1,128)}, f32[192,128]{1,0:T(8,128)}, f32[192,128]{1,0:T(8,128)}, f32[192,2048]{1,0:T(8,128)}) custom-call(f32[1,128]{1,0:T(1,128)} %get-tuple-element.12.refs_0_, f32[192,128]{1,0:T(8,128)} %get-tuple-element.13.refs_1_, f32[192,128]{1,0:T(8,128)} %get-tuple-element.14.refs_2_, f32[192,2048]{1,0:T(8,128)} %get-tuple-element.15.refs_3_), custom_call_target="tpu_custom_call" | custom-call | tf_op jit(solution)/shard_map/results/pallas_call | solution.py:781
